TPU v7x, 128 devices: a whole 4x4x4 slice. The times are simulated.
128 devices in a mesh: blk: 32 (over x, y, z_hi), walk: 4 (over z_lo, core).
Axes of the slice: x: 4, y: 4, z: 4 (z_hi: 2, z_lo: 2; z = z_hi * 2 + z_lo), core: 2. Of those that a mesh axis runs over, the one named last changes fastest.
Arguments:
- walker_m: bfloat16 [4, 32, 128, 128], P('walk', 'blk'), may hold values from -6 to 6
- vertex_times: int32 [4, 32, 128], P('walk', 'blk'), may hold values from 0 to 1023
- vertex_labels: int32 [4, 32, 128], P('walk', 'blk'), may hold values from 0 to 35
- freq_index: int32 [24], replicated, may hold values from -64 to 63
- q_index: int32 [32], P('blk'), may hold values from 0 to 35
Outputs:
- g4: float32 [32, 2, 864, 864], P('blk', None, 'walk')
Inputs may be any that keep to these rules, and one draw needn't show every extreme that they name: `q_index`: entry b is 6 qx + qy for the transfer momentum (qx, qy). `freq_index`: frequency f is pi (2 n + 1) / beta with n its entry. `vertex_times`: the time is entry * beta / 1024. `vertex_labels`: site s lies at row s // 6 and column s mod 6 of the 6×6 cluster.
All inputs are finite; a program needn't handle non-finite values.
Results may differ from a plain program's by a relative error of at most 0.0061.
Values may be sent and summed in bfloat16 or wider, within the bound.
No kernel may reach another device: no remote copies, remote signals or barrier semaphores. Data moves between devices by JAX's collectives and lax.ppermute only.
A program may use at most 128 MiB of HBM per device.

v0:
```python
import math

import jax
import jax.numpy as jnp
from jax import lax
from jax.sharding import PartitionSpec as P

SIDE = 6
NF = 24
K = 864
V = 128
STEPS = 4
TGRID = 1024


TWO_PI = 2.0 * math.pi


def from_behind(value, axis, steps):
    count = lax.axis_size(axis)
    pairs = [(source, (source + steps) % count) for source in range(count)]
    return lax.ppermute(value, axis, pairs)


def phase_tables(time_points, labels, frequencies):
    modulus = 12 * TGRID
    momenta = jnp.arange(SIDE * SIDE, dtype=jnp.int32)
    momentum_across = momenta // SIDE
    momentum_down = momenta % SIDE
    site_across = labels // SIDE
    site_down = labels % SIDE
    freq_part = jnp.mod((2 * frequencies[:, None] + 1) * time_points[None, :] * 6, modulus)
    momentum_part = jnp.mod(
        2
        * TGRID
        * (
            momentum_across[:, None] * site_across[None, :]
            + momentum_down[:, None] * site_down[None, :]
        ),
        modulus,
    )
    phase = jnp.mod(freq_part[None, :, :] - momentum_part[:, None, :], modulus).reshape(
        SIDE * SIDE * NF, -1
    )
    angles = phase.astype(jnp.float32) * (TWO_PI / modulus)
    return (jnp.cos(angles).astype(jnp.bfloat16), jnp.sin(angles).astype(jnp.bfloat16))


def amplitudes(matrix, time_points, labels, frequencies):
    cos_table, sin_table = phase_tables(time_points, labels, frequencies)
    stacked = jnp.concatenate([cos_table, sin_table], axis=0)
    amplitude = jnp.dot(stacked, matrix, preferred_element_type=jnp.float32).astype(jnp.bfloat16)
    right_side = jnp.concatenate([cos_table, sin_table], axis=1)
    return (amplitude[:K], amplitude[K:], right_side)


def complex_left(real_part, imag_part):
    return jnp.concatenate(
        [
            jnp.concatenate([real_part, imag_part], axis=1),
            jnp.concatenate([imag_part, -real_part], axis=1),
        ],
        axis=0,
    )


def green_product(left_side, right_side, row_count, col_count):
    table = lax.dot_general(
        left_side, right_side, (((1,), (1,)), ((), ())), preferred_element_type=jnp.float32
    )
    return (table * (1.0 / V)).reshape(2, row_count, col_count)


def walker_term(matrix, time_points, labels, frequencies, shifted):
    real_part, imag_part, right_side = amplitudes(matrix, time_points, labels, frequencies)
    green_table = green_product(complex_left(real_part, imag_part), right_side, K, K)
    moved_left = complex_left(
        jnp.take(real_part, shifted, axis=0), jnp.take(imag_part, shifted, axis=0)
    )
    shifted_green = green_product(moved_left, jnp.take(right_side, shifted, axis=0), K, K)
    flipped = jnp.swapaxes(green_table, 1, 2)
    real_term = shifted_green[0] * flipped[0] - shifted_green[1] * flipped[1]
    imag_term = shifted_green[0] * flipped[1] + shifted_green[1] * flipped[0]
    return jnp.stack([real_term, imag_term])


def shifted_rows(transfer):
    row_index = jnp.arange(K, dtype=jnp.int32)
    momentum = row_index // NF
    offset = row_index % NF
    shift_across = (momentum // SIDE + transfer // SIDE) % SIDE
    shift_down = (momentum % SIDE + transfer % SIDE) % SIDE
    return (shift_across * SIDE + shift_down) * NF + offset


def settle(running, first_half, finished, half_window):
    if finished == half_window:
        first_half = lax.psum_scatter(running[None], "walk", scatter_dimension=2, tiled=True)
        running = jnp.zeros_like(running)
    return (running, first_half)


def local(walker_m, vertex_times, vertex_labels, freq_index, q_index):
    group_count = lax.axis_size("walk")
    half_window = STEPS // 2
    shifted = shifted_rows(q_index[0])
    first_half = None
    held = (walker_m, vertex_times, vertex_labels)
    running = jnp.zeros((2, K, K), jnp.float32)
    own_walker = (held[0][:, 0], held[1][:, 0], held[2][:, 0])

    def absorb(running, walker):
        running = running + walker_term(
            walker[0][0], walker[1][0], walker[2][0], freq_index, shifted
        )
        return running

    forward = own_walker
    backward = own_walker
    running = absorb(running, own_walker)
    running, first_half = settle(running, first_half, 1, half_window)
    for number in range(1, STEPS):
        if number % 2 == 1:
            forward = from_behind((forward[0], forward[1], forward[2]), "blk", -1)
            walker = forward
        else:
            backward = from_behind((backward[0], backward[1], backward[2]), "blk", 1)
            walker = backward
        running = absorb(running, walker)
        running, first_half = settle(running, first_half, number + 1, half_window)
    summed = first_half + lax.psum_scatter(running[None], "walk", scatter_dimension=2, tiled=True)
    return summed * (1.0 / (STEPS * group_count))


def solution(mesh):
    return jax.shard_map(
        local,
        mesh=mesh,
        in_specs=(
            P("walk", "blk", None, None),
            P("walk", "blk", None),
            P("walk", "blk", None),
            P(),
            P("blk"),
        ),
        out_specs=P("blk", None, "walk", None),
        check_vma=False,
    )
```

profile of v0, /device:TPU:1, one launch (start us, length us, event | category | flops | bytes accessed | tf_op | source)
XLA Modules:
  0.0 243.3 jit_solution(4178816977162463180)
XLA Ops:
  6.5 9.1 %collective-permute-start.1 = (s32[1,128]{1,0:T(1,128)}, s32[1,128]{1,0:T(1,128)S(1)}, u32[]{:S(2)}, u32[]{:S(2)}) collective-permute-start(s32[1,128]{1,0:T(1,128)} %bitcast.195), channel_id=1, source_target_pairs={{0,124},{4,0},{8,4},{12,8},{16,12},{20,16},{24,20},{28,24},{32,28}... | collective-permute-start | bytes 1544 | tf_op jit(solution)/shard_map/ppermute | solution.py:22
  15.6 7.2 %collective-permute-start = (s32[1,128]{1,0:T(1,128)}, s32[1,128]{1,0:T(1,128)S(1)}, u32[]{:S(2)}, u32[]{:S(2)}) collective-permute-start(s32[1,128]{1,0:T(1,128)} %bitcast.189), channel_id=1, source_target_pairs={{0,124},{4,0},{8,4},{12,8},{16,12},{20,16},{24,20},{28,24},{32,28}... | collective-permute-start | bytes 1544 | tf_op jit(solution)/shard_map/ppermute | solution.py:22
  22.8 7.2 %collective-permute-start.2 = (bf16[1,128,128]{2,1,0:T(8,128)(2,1)}, bf16[1,128,128]{2,1,0:T(8,128)(2,1)}, u32[]{:S(2)}, u32[]{:S(2)}) collective-permute-start(bf16[1,128,128]{2,1,0:T(8,128)(2,1)} %bitcast.187), channel_id=1, source_target_pairs={{0,124},{4,0},{8,4},{12,8},{16,12},{20,16},{24,20},{28,24},{32,28}... | collective-permute-start | bytes 98312 | tf_op jit(solution)/shard_map/ppermute | solution.py:22
  32.2 7.2 %collective-permute-start.7 = (s32[1,128]{1,0:T(1,128)S(1)}, s32[1,128]{1,0:T(1,128)S(1)}, u32[]{:S(2)}, u32[]{:S(2)}) collective-permute-start(s32[1,128]{1,0:T(1,128)S(1)} %collective-permute-done.1), channel_id=1, source_target_pairs={{0,124},{4,0},{8,4},{12,8},{16,12},{20,16},{24,20},{28,24},{32,28}... | collective-permute-start | bytes 1544 | tf_op jit(solution)/shard_map/ppermute | solution.py:22
  39.8 4.0 %collective-permute-done.6 = s32[1,128]{1,0:T(1,128)S(1)} collective-permute-done((s32[1,128]{1,0:T(1,128)S(1)}, s32[1,128]{1,0:T(1,128)S(1)}, u32[]{:S(2)}, u32[]{:S(2)}) %collective-permute-start.6) | collective-permute-done | bytes 544 | tf_op jit(solution)/shard_map/ppermute | solution.py:22
  53.6 3.7 %convolution_multiply_fusion.6 = f32[1728,864]{1,0:T(8,128)} fusion(bf16[864,128]{1,0:T(8,128)(2,1)S(1)} %get-tuple-element.39, bf16[864,128]{1,0:T(8,128)(2,1)S(1)} %get-tuple-element.40, bf16[864,128]{1,0:T(8,128)(2,1)S(1)} %get-tuple-element.38, bf16[864,128]{1,0:T(8,128)(2,1)S(1)} %get-tuple-element.42, bf16[864,128]{1,0:T(8,128)(2,1)S(1)} %get-tuple-element.41), kind=kOutput, calls=%fused_computation.21 | convolution fusion | flops 770328576 | bytes 7077888 | tf_op jit(solution)/shard_map/dot_general | solution.py:68
  57.4 3.0 %gather_fusion = bf16[864,128]{1,0:T(8,128)(2,1)} fusion(bf16[864,128]{1,0:T(8,128)(2,1)S(1)} %get-tuple-element.38, s32[1024]{0:T(1024)S(1)} %pad_clamp_fusion), kind=kCustom, calls=%fused_computation.clone | custom fusion | bytes 445824 | tf_op jit(solution)/shard_map/jit(_take)/gather | solution.py:78
  63.5 3.5 %gather_fusion.11 = bf16[864,256]{1,0:T(8,128)(2,1)S(1)} fusion(bf16[864,256]{1,0:T(8,128)(2,1)S(1)} %pad_maximum_fusion.3, s32[1024]{0:T(1024)S(1)} %pad_clamp_fusion), kind=kCustom, calls=%fused_computation.11.clone | custom fusion | bytes 888192 | tf_op jit(solution)/shard_map/jit(_take)/gather | solution.py:80
  66.9 3.9 %gather_fusion.8 = bf16[864,256]{1,0:T(8,128)(2,1)} fusion(bf16[864,256]{1,0:T(8,128)(2,1)S(1)} %pad_maximum_fusion.2, s32[1024]{0:T(1024)S(1)} %pad_clamp_fusion), kind=kCustom, calls=%fused_computation.10.clone | custom fusion | bytes 888192 | tf_op jit(solution)/shard_map/jit(_take)/gather | solution.py:80
  70.9 3.9 %gather_fusion.5 = bf16[864,256]{1,0:T(8,128)(2,1)} fusion(bf16[864,256]{1,0:T(8,128)(2,1)S(1)} %pad_maximum_fusion.1, s32[1024]{0:T(1024)S(1)} %pad_clamp_fusion), kind=kCustom, calls=%fused_computation.9.clone | custom fusion | bytes 888192 | tf_op jit(solution)/shard_map/jit(_take)/gather | solution.py:80
  74.8 3.9 %gather_fusion.2 = bf16[864,256]{1,0:T(8,128)(2,1)} fusion(bf16[864,256]{1,0:T(8,128)(2,1)S(1)} %pad_maximum_fusion, s32[1024]{0:T(1024)S(1)} %pad_clamp_fusion), kind=kCustom, calls=%fused_computation.1.clone | custom fusion | bytes 888192 | tf_op jit(solution)/shard_map/jit(_take)/gather | solution.py:80
  78.7 7.3 %copy.6 = f32[2,864,864]{1,2,0:T(8,128)} copy(f32[2,864,864]{2,1,0:T(8,128)} %bitcast.172) | data formatting | bytes 11943936 | tf_op jit(solution)/shard_map/reshape | solution.py:71
  88.3 3.7 %convolution_multiply_fusion.2 = f32[1728,864]{1,0:T(8,128)} fusion(bf16[864,128]{1,0:T(8,128)(2,1)S(1)} %get-tuple-element.29, bf16[864,128]{1,0:T(8,128)(2,1)S(1)} %get-tuple-element.30, bf16[864,128]{1,0:T(8,128)(2,1)S(1)} %get-tuple-element.28, bf16[864,128]{1,0:T(8,128)(2,1)S(1)} %get-tuple-element.32, bf16[864,128]{1,0:T(8,128)(2,1)S(1)} %get-tuple-element.31), kind=kOutput, calls=%fused_computation.17 | convolution fusion | flops 770328576 | bytes 7077888 | tf_op jit(solution)/shard_map/dot_general | solution.py:68
  92.0 4.1 %collective-permute-start.8 = (bf16[1,128,128]{2,1,0:T(8,128)(2,1)}, bf16[1,128,128]{2,1,0:T(8,128)(2,1)S(1)}, u32[]{:S(2)}, u32[]{:S(2)}) collective-permute-start(bf16[1,128,128]{2,1,0:T(8,128)(2,1)} %collective-permute-done.2), channel_id=1, source_target_pairs={{0,124},{4,0},{8,4},{12,8},{16,12},{20,16},{24,20},{28,24},{32,28}... | collective-permute-start | bytes 98312 | tf_op jit(solution)/shard_map/ppermute | solution.py:22
  96.1 3.7 %convolution_multiply_fusion.4 = f32[1728,864]{1,0:T(8,128)} fusion(bf16[864,128]{1,0:T(8,128)(2,1)S(1)} %get-tuple-element.34, bf16[864,128]{1,0:T(8,128)(2,1)S(1)} %get-tuple-element.35, bf16[864,128]{1,0:T(8,128)(2,1)S(1)} %get-tuple-element.33, bf16[864,128]{1,0:T(8,128)(2,1)S(1)} %get-tuple-element.37, bf16[864,128]{1,0:T(8,128)(2,1)S(1)} %get-tuple-element.36), kind=kOutput, calls=%fused_computation.19 | convolution fusion | flops 770328576 | bytes 7077888 | tf_op jit(solution)/shard_map/dot_general | solution.py:68
  109.3 7.3 %copy.8 = f32[2,864,864]{1,2,0:T(8,128)} copy(f32[2,864,864]{2,1,0:T(8,128)} %bitcast.171) | data formatting | bytes 11943936 | tf_op jit(solution)/shard_map/reshape | solution.py:71
  116.6 7.3 %copy.7 = f32[2,864,864]{1,2,0:T(8,128)} copy(f32[2,864,864]{2,1,0:T(8,128)} %bitcast.173) | data formatting | bytes 11943936 | tf_op jit(solution)/shard_map/reshape | solution.py:71
  129.0 3.8 %convolution_multiply_fusion = f32[1728,864]{1,0:T(8,128)} fusion(bf16[864,128]{1,0:T(8,128)(2,1)S(1)} %get-tuple-element.24, bf16[864,128]{1,0:T(8,128)(2,1)S(1)} %get-tuple-element.25, bf16[864,128]{1,0:T(8,128)(2,1)S(1)} %get-tuple-element.23, bf16[864,128]{1,0:T(8,128)(2,1)S(1)} %get-tuple-element.27, bf16[864,128]{1,0:T(8,128)(2,1)S(1)} %get-tuple-element.26), kind=kOutput, calls=%fused_computation.15 | convolution fusion | flops 770328576 | bytes 7077888 | tf_op jit(solution)/shard_map/dot_general | solution.py:68
  132.8 7.4 %copy.9 = f32[2,864,864]{1,2,0:T(8,128)} copy(f32[2,864,864]{2,1,0:T(8,128)} %bitcast.174) | data formatting | bytes 11943936 | tf_op jit(solution)/shard_map/reshape | solution.py:71
  148.6 3.2 %subtract_bitcast_fusion.1 = (f32[1,1,864,864]{3,2,1,0:T(8,128)}, f32[1,1,864,864]{3,2,1,0:T(8,128)}) fusion(f32[2,864,864]{2,1,0:T(8,128)S(1)} %bitcast.183, f32[1728,864]{1,0:T(8,128)S(1)} %convolution_multiply_fusion.3), kind=kLoop, calls=%fused_computation.34 | loop fusion | flops 4478976 | bytes 17915904 | tf_op jit(solution)/shard_map/stack | solution.py:84
  155.0 3.2 %subtract_bitcast_fusion.2 = (f32[1,1,864,864]{3,2,1,0:T(8,128)}, f32[1,1,864,864]{3,2,1,0:T(8,128)}) fusion(f32[2,864,864]{2,1,0:T(8,128)S(1)} %bitcast.180, f32[1728,864]{1,0:T(8,128)S(1)} %convolution_multiply_fusion.5), kind=kLoop, calls=%fused_computation.36 | loop fusion | flops 4478976 | bytes 17915904 | tf_op jit(solution)/shard_map/stack | solution.py:84
  161.3 3.3 %subtract_bitcast_fusion.3 = (f32[1,1,864,864]{3,2,1,0:T(8,128)}, f32[1,1,864,864]{3,2,1,0:T(8,128)}) fusion(f32[2,864,864]{2,1,0:T(8,128)S(1)} %bitcast.177, f32[1728,864]{1,0:T(8,128)S(1)} %convolution_multiply_fusion.7), kind=kLoop, calls=%fused_computation.38 | loop fusion | flops 4478976 | bytes 17915904 | tf_op jit(solution)/shard_map/stack | solution.py:84
  164.5 9.8 %fusion = f32[1,2,864,864]{3,2,1,0:T(8,128)} fusion(f32[1,1,864,864]{3,2,1,0:T(8,128)} %get-tuple-element.22, f32[1,1,864,864]{3,2,1,0:T(8,128)} %get-tuple-element.21, f32[1,1,864,864]{3,2,1,0:T(8,128)} %get-tuple-element.20, f32[1,1,864,864]{3,2,1,0:T(8,128)} %get-tuple-element.19, f32[1,1,864,864]{3,2,1,0:T(8,128)} %get-tuple-element.18, ...), kind=kLoop, calls=%fused_computation.13 | loop fusion | flops 10450944 | bytes 29859840 | tf_op jit(solution)/shard_map/add | solution.py:131
  174.3 59.5 %reduce-scatter.2.cloned.1.call-done = f32[1,2,216,864]{3,2,1,0:T(8,128)} async-done(((f32[1,2,864,864]{3,2,1,0:T(8,128)}), f32[1,2,216,864]{3,2,1,0:T(8,128)}) %reduce-scatter.2.cloned.1.call-update) | async-done | bytes 1493008 | tf_op jit(solution)/shard_map/reduce_scatter | solution.py:98
  (88 shorter events, 48.6 us)
Async XLA Ops:
  6.5 227.3 %reduce-scatter.2.cloned.1.call-start = ((), (), s32[]{:S(2)}) async-start(), calls=%async_computation.1 | async-start | bytes 7741440 | tf_op jit(solution)/shard_map/reduce_scatter | solution.py:98
  6.5 25.6 %collective-permute-start.1 = (s32[1,128]{1,0:T(1,128)}, s32[1,128]{1,0:T(1,128)S(1)}, u32[]{:S(2)}, u32[]{:S(2)}) collective-permute-start(s32[1,128]{1,0:T(1,128)} %bitcast.195), channel_id=1, source_target_pairs={{0,124},{4,0},{8,4},{12,8},{16,12},{20,16},{24,20},{28,24},{32,28}... | collective-permute-start | bytes 1544 | tf_op jit(solution)/shard_map/ppermute | solution.py:22
  15.6 16.6 %collective-permute-start.4 = (s32[1,128]{1,0:T(1,128)}, s32[1,128]{1,0:T(1,128)S(1)}, u32[]{:S(2)}, u32[]{:S(2)}) collective-permute-start(s32[1,128]{1,0:T(1,128)} %bitcast.196), channel_id=1, source_target_pairs={{0,4},{4,8},{8,12},{12,16},{16,20},{20,24},{24,28},{28,32},{32,36}... | collective-permute-start | bytes 1544 | tf_op jit(solution)/shard_map/ppermute | solution.py:22
  15.6 23.9 %collective-permute-start = (s32[1,128]{1,0:T(1,128)}, s32[1,128]{1,0:T(1,128)S(1)}, u32[]{:S(2)}, u32[]{:S(2)}) collective-permute-start(s32[1,128]{1,0:T(1,128)} %bitcast.189), channel_id=1, source_target_pairs={{0,124},{4,0},{8,4},{12,8},{16,12},{20,16},{24,20},{28,24},{32,28}... | collective-permute-start | bytes 1544 | tf_op jit(solution)/shard_map/ppermute | solution.py:22
  22.8 17.0 %collective-permute-start.3 = (s32[1,128]{1,0:T(1,128)}, s32[1,128]{1,0:T(1,128)S(1)}, u32[]{:S(2)}, u32[]{:S(2)}) collective-permute-start(s32[1,128]{1,0:T(1,128)} %bitcast.190), channel_id=1, source_target_pairs={{0,4},{4,8},{8,12},{12,16},{16,20},{20,24},{24,28},{28,32},{32,36}... | collective-permute-start | bytes 1544 | tf_op jit(solution)/shard_map/ppermute | solution.py:22
  22.8 63.3 %collective-permute-start.2 = (bf16[1,128,128]{2,1,0:T(8,128)(2,1)}, bf16[1,128,128]{2,1,0:T(8,128)(2,1)}, u32[]{:S(2)}, u32[]{:S(2)}) collective-permute-start(bf16[1,128,128]{2,1,0:T(8,128)(2,1)} %bitcast.187), channel_id=1, source_target_pairs={{0,124},{4,0},{8,4},{12,8},{16,12},{20,16},{24,20},{28,24},{32,28}... | collective-permute-start | bytes 98312 | tf_op jit(solution)/shard_map/ppermute | solution.py:22
  32.1 55.0 %collective-permute-start.5 = (bf16[1,128,128]{2,1,0:T(8,128)(2,1)}, bf16[1,128,128]{2,1,0:T(8,128)(2,1)}, u32[]{:S(2)}, u32[]{:S(2)}) collective-permute-start(bf16[1,128,128]{2,1,0:T(8,128)(2,1)} %bitcast.188), channel_id=1, source_target_pairs={{0,4},{4,8},{8,12},{12,16},{16,20},{20,24},{24,28},{28,32},{32,36}... | collective-permute-start | bytes 98312 | tf_op jit(solution)/shard_map/ppermute | solution.py:22
  32.2 12.3 %collective-permute-start.7 = (s32[1,128]{1,0:T(1,128)S(1)}, s32[1,128]{1,0:T(1,128)S(1)}, u32[]{:S(2)}, u32[]{:S(2)}) collective-permute-start(s32[1,128]{1,0:T(1,128)S(1)} %collective-permute-done.1), channel_id=1, source_target_pairs={{0,124},{4,0},{8,4},{12,8},{16,12},{20,16},{24,20},{28,24},{32,28}... | collective-permute-start | bytes 1544 | tf_op jit(solution)/shard_map/ppermute | solution.py:22
  39.5 4.3 %collective-permute-start.6 = (s32[1,128]{1,0:T(1,128)S(1)}, s32[1,128]{1,0:T(1,128)S(1)}, u32[]{:S(2)}, u32[]{:S(2)}) collective-permute-start(s32[1,128]{1,0:T(1,128)S(1)} %collective-permute-done), channel_id=1, source_target_pairs={{0,124},{4,0},{8,4},{12,8},{16,12},{20,16},{24,20},{28,24},{32,28}... | collective-permute-start | bytes 1544 | tf_op jit(solution)/shard_map/ppermute | solution.py:22
  92.0 31.9 %collective-permute-start.8 = (bf16[1,128,128]{2,1,0:T(8,128)(2,1)}, bf16[1,128,128]{2,1,0:T(8,128)(2,1)S(1)}, u32[]{:S(2)}, u32[]{:S(2)}) collective-permute-start(bf16[1,128,128]{2,1,0:T(8,128)(2,1)} %collective-permute-done.2), channel_id=1, source_target_pairs={{0,124},{4,0},{8,4},{12,8},{16,12},{20,16},{24,20},{28,24},{32,28}... | collective-permute-start | bytes 98312 | tf_op jit(solution)/shard_map/ppermute | solution.py:22
  132.8 7.4 %copy-start.3 = (bf16[864,128]{1,0:T(8,128)(2,1)S(1)}, bf16[864,128]{1,0:T(8,128)(2,1)}, u32[]{:S(2)}) copy-start(bf16[864,128]{1,0:T(8,128)(2,1)} %gather_fusion) | copy-start | bytes 663556
  132.8 7.4 %copy-start.4 = (bf16[864,128]{1,0:T(8,128)(2,1)S(1)}, bf16[864,128]{1,0:T(8,128)(2,1)}, u32[]{:S(2)}) copy-start(bf16[864,128]{1,0:T(8,128)(2,1)} %gather_fusion.1) | copy-start | bytes 663556
  141.8 2.2 slice-start.6
  141.8 2.8 %slice-start.7 = ((s8[6193152]{0:T(1024)(128)(4,1)}), s8[1998848]{0:T(1024)(128)(4,1)S(1)}, s32[]{:S(2)}) async-start(s8[6193152]{0:T(1024)(128)(4,1)} %bitcast.184), calls=%async_computation.9 | async-start | bytes 3997696
  144.6 1.0 copy-start.2
  145.2 3.0 %slice-start.4 = ((s8[6193152]{0:T(1024)(128)(4,1)}), s8[4194304]{0:T(1024)(128)(4,1)S(1)}, s32[]{:S(2)}) async-start(s8[6193152]{0:T(1024)(128)(4,1)} %bitcast.181), calls=%async_computation.6 | async-start | bytes 8388608
  145.6 2.9 %slice-start.5 = ((s8[6193152]{0:T(1024)(128)(4,1)}), s8[1998848]{0:T(1024)(128)(4,1)S(1)}, s32[]{:S(2)}) async-start(s8[6193152]{0:T(1024)(128)(4,1)} %bitcast.181), calls=%async_computation.7 | async-start | bytes 3997696
  148.5 3.2 %copy-start.1 = (bf16[864,256]{1,0:T(8,128)(2,1)S(1)}, bf16[864,256]{1,0:T(8,128)(2,1)}, u32[]{:S(2)}) copy-start(bf16[864,256]{1,0:T(8,128)(2,1)} %gather_fusion.5) | copy-start | bytes 1327108
  151.8 2.6 %slice-start.2 = ((s8[6193152]{0:T(1024)(128)(4,1)}), s8[4194304]{0:T(1024)(128)(4,1)S(1)}, s32[]{:S(2)}) async-start(s8[6193152]{0:T(1024)(128)(4,1)} %bitcast.178), calls=%async_computation.4 | async-start | bytes 8388608
  151.8 3.2 %slice-start.3 = ((s8[6193152]{0:T(1024)(128)(4,1)}), s8[1998848]{0:T(1024)(128)(4,1)S(1)}, s32[]{:S(2)}) async-start(s8[6193152]{0:T(1024)(128)(4,1)} %bitcast.178), calls=%async_computation.5 | async-start | bytes 3997696
  155.0 3.3 %copy-start = (bf16[864,256]{1,0:T(8,128)(2,1)S(1)}, bf16[864,256]{1,0:T(8,128)(2,1)}, u32[]{:S(2)}) copy-start(bf16[864,256]{1,0:T(8,128)(2,1)} %gather_fusion.2) | copy-start | bytes 1327108
  158.2 2.4 slice-start
  158.2 3.0 %slice-start.1 = ((s8[6193152]{0:T(1024)(128)(4,1)}), s8[1998848]{0:T(1024)(128)(4,1)S(1)}, s32[]{:S(2)}) async-start(s8[6193152]{0:T(1024)(128)(4,1)} %bitcast.175), calls=%async_computation.3 | async-start | bytes 3997696
Sparse Core Ops, SparseCore 0:
  174.4 59.3 reduce-scatter.1
where the time goes:
time: 244 us; the launch traced here: 243 us
  local copies, waits for them, and re-layouts  68.3 us (28%)
  waiting for transfers between devices  63.6 us (26%)
  starting transfers between devices  35.1 us (14%)
  other arithmetic  34.7 us (14%)
  matrix products  27.2 us (11%)
  between operations  14.4 us (6%)
    reduce_scatter x1, waiting for transfers between devices, settle(): lax.psum_scatter(running[None], 'walk', scatter_dimension=2, tiled=True)  59.5 us
    ppermute x9, starting transfers between devices, from_behind(): return lax.ppermute(value, axis, pairs)  35.1 us
    reshape x4, local copies, waits for them, and re-layouts, green_product(): return (table * (1.0 / V)).reshape(2, row_count, col_count)  29.2 us
    dot_general x8, matrix products, green_product(): lax.dot_general(left_side, right_side, (((1,), (1,)), ((), ())), preferre...  23.8 us
    gather x4, local copies, waits for them, and re-layouts, walker_term(): jnp.take(right_side, shifted, axis=0)  15.3 us
    another operation x4, other arithmetic, walker_term(): return jnp.stack([real_term, imag_term])  10.4 us
    gather x4, local copies, waits for them, and re-layouts, walker_term(): jnp.take(imag_part, shifted, axis=0)  10.2 us
    gather x4, local copies, waits for them, and re-layouts, walker_term(): jnp.take(real_part, shifted, axis=0)  10.2 us
  transfers between devices with their start and end apart: 10, of which 2 were waited for; matrix products, arithmetic and copies ran while one was open for 30% of the time, Pallas kernels for 0%

commit v1 on v0

v1 whole, which is shorter than its diff:
```python
import jax
import jax.numpy as jnp
from jax import lax
from jax.experimental import pallas as pl
from jax.experimental.pallas import tpu as pltpu
from jax.sharding import PartitionSpec as P

SIDE = 6
NF = 24
K = 864
V = 128
STEPS = 4
ROWS = 216
PACK = 144
BLOCKS = 9
COL_TILES = ((0, 256), (256, 256), (512, 256), (768, 96))


def quarter_cos_sin(turns):
    near = jnp.floor(turns + 0.5)
    x = turns - near
    x2 = x * x
    s = x * (1.5707963267948966 + x2 * (-0.6459640975062462 + x2 * (0.07969262624616704 + x2 * (-0.004681754135318688 + x2 * 0.00016044118478735982))))
    c = 1.0 + x2 * (-1.2337005501361697 + x2 * (0.253669507901048 + x2 * (-0.02086348076335296 + x2 * (0.0009192602748394266 + x2 * -2.520204237306061e-05))))
    quad = near - 4.0 * jnp.floor(near * 0.25)
    odd = (quad == 1.0) | (quad == 3.0)
    cc = jnp.where(odd, s, c)
    ss = jnp.where(odd, c, s)
    cc = jnp.where((quad == 1.0) | (quad == 2.0), -cc, cc)
    ss = jnp.where(quad >= 2.0, -ss, ss)
    return cc, ss


def sixth_cos_sin(m):
    y = m - 6.0 * jnp.floor((m + 0.5) * (1.0 / 6.0))
    z = jnp.abs(y - 3.0)
    half = 0.8660254037844386
    c = jnp.where(z == 3.0, 1.0, jnp.where(z == 2.0, 0.5, jnp.where(z == 1.0, -0.5, -1.0)))
    s = jnp.where((z == 3.0) | (z == 0.0), 0.0, jnp.where(y < 3.0, half, -half))
    return c, s


def walker_kernel(place_ref, odd_freq_ref, walkers_ref, out_ref, table_ref, left_ref):
    step = pl.program_id(0)
    share, transfer = place_ref[0], place_ref[1]
    packed = walkers_ref[0]
    meta = packed[V:, :].astype(jnp.float32)
    times = meta[0:1] * 32.0 + meta[1:2]
    sites = meta[2:3]
    site_x = jnp.floor((sites + 0.5) * (1.0 / SIDE))
    site_y = sites - SIDE * site_x
    product = odd_freq_ref[...] * times
    freq_c, freq_s = quarter_cos_sin((product - 2048.0 * jnp.floor(product * (1.0 / 2048.0))) * (1.0 / 512.0))

    def rows_of(kx, ky):
        return sixth_cos_sin(kx * site_x + ky * site_y)

    index = lax.broadcasted_iota(jnp.int32, (16, V), 0)
    base_c, base_s = rows_of((index // 3).astype(jnp.float32), (index % 3).astype(jnp.float32))
    mine = index + BLOCKS * share
    mine_x = (mine // SIDE).astype(jnp.float32)
    mine_y = (mine % SIDE).astype(jnp.float32)
    q_x = (transfer // SIDE).astype(jnp.float32)
    q_y = (transfer % SIDE).astype(jnp.float32)
    mine_c, mine_s = rows_of(mine_x, mine_y)
    moved_c, moved_s = rows_of(mine_x + q_x, mine_y + q_y)
    turn_c, turn_s = rows_of(q_x, q_y)
    flip_x = 1.0 - 2.0 * (site_x - 2.0 * jnp.floor(site_x * 0.5))
    flip_y = 1.0 - 2.0 * (site_y - 2.0 * jnp.floor(site_y * 0.5))

    def rotated(c, s, row):
        c, s = c[row : row + 1], s[row : row + 1]
        return freq_c * c + freq_s * s, freq_s * c - freq_c * s

    for kx in range(3):
        blocks = [rotated(base_c, base_s, 3 * kx + ky) for ky in range(3)]
        blocks = blocks + [(c * flip_y, s * flip_y) for c, s in blocks]
        cos_part = jnp.concatenate([b[0] for b in blocks], axis=0).astype(jnp.bfloat16)
        sin_part = jnp.concatenate([b[1] for b in blocks], axis=0).astype(jnp.bfloat16)
        flip = flip_x.astype(jnp.bfloat16)
        table_ref[pl.ds(144 * kx, 144), 0:V] = cos_part
        table_ref[pl.ds(144 * kx, 144), V:] = sin_part
        table_ref[pl.ds(144 * (kx + 3), 144), 0:V] = cos_part * flip
        table_ref[pl.ds(144 * (kx + 3), 144), V:] = sin_part * flip

    def stacked(c, s):
        blocks = [rotated(c, s, j) for j in range(BLOCKS)]
        return jnp.concatenate([b[0] for b in blocks] + [b[1] for b in blocks], axis=0).astype(jnp.bfloat16)

    matrix = packed[:V, :]
    first = jnp.dot(stacked(moved_c, moved_s), matrix, preferred_element_type=jnp.float32)
    second = lax.dot_general(stacked(mine_c, mine_s), matrix, (((1,), (1,)), ((), ())), preferred_element_type=jnp.float32)
    a_re, a_im = first[:ROWS], first[ROWS:]
    turn_c, turn_s = turn_c[0:1], turn_s[0:1]
    a_re, a_im = a_re * turn_c - a_im * turn_s, a_re * turn_s + a_im * turn_c
    b_re, b_im = second[:ROWS], second[ROWS:]

    def interleave(parts):
        return jnp.stack([p.reshape(27, 8, V) for p in parts], axis=1).reshape(K, V).astype(jnp.bfloat16)

    left_ref[:, 0:V] = interleave([a_re, a_im, b_re, -b_im])
    left_ref[:, V:] = interleave([a_im, -a_re, b_im, b_re])

    @pl.when(step == 0)
    def _():
        out_ref[...] = jnp.zeros_like(out_ref)

    for start, size in COL_TILES:
        product = lax.dot_general(left_ref[...], table_ref[pl.ds(start, size), :], (((1,), (1,)), ((), ())), preferred_element_type=jnp.float32)
        product = product.reshape(27, 4, 8, size)
        m_re, m_im, n_re, n_im = (product[:, i] for i in range(4))
        out_ref[0, :, pl.ds(start, size)] += (m_re * n_re - m_im * n_im).reshape(ROWS, size)
        out_ref[1, :, pl.ds(start, size)] += (m_re * n_im + m_im * n_re).reshape(ROWS, size)

    @pl.when(step == pl.num_programs(0) - 1)
    def _():
        out_ref[...] = out_ref[...] * (2.0 ** -18)


def accumulate(place, odd_freq, walkers):
    return pl.pallas_call(
        walker_kernel,
        out_shape=jax.ShapeDtypeStruct((2, ROWS, K), jnp.float32),
        grid_spec=pltpu.PrefetchScalarGridSpec(
            num_scalar_prefetch=1,
            grid=(walkers.shape[0],),
            in_specs=[
                pl.BlockSpec((NF, V), lambda i, p: (0, 0)),
                pl.BlockSpec((1, PACK, V), lambda i, p: (i, 0, 0)),
            ],
            out_specs=pl.BlockSpec((2, ROWS, K), lambda i, p: (0, 0, 0)),
            scratch_shapes=[pltpu.VMEM((K, 256), jnp.bfloat16), pltpu.VMEM((K, 256), jnp.bfloat16)],
        ),
        compiler_params=pltpu.CompilerParams(vmem_limit_bytes=48 << 20),
    )(place, odd_freq, walkers)


def shifted_owner(value, steps):
    count = lax.axis_size("blk")
    return lax.ppermute(value, "blk", [((i + steps) % count, i) for i in range(count)])


def local(walker_m, vertex_times, vertex_labels, freq_index, q_index):
    times, labels = vertex_times[0], vertex_labels[0]
    meta = jnp.concatenate([times // 32, times % 32, labels], axis=0).astype(jnp.bfloat16)
    packed = jnp.concatenate([walker_m[0, 0], meta, jnp.zeros((PACK - V - 3, V), jnp.bfloat16)], axis=0)
    groups = lax.all_gather(packed, "walk", axis=0)
    walkers = jnp.concatenate([groups] + [shifted_owner(groups, d) for d in (-1, 1, 2)], axis=0)
    place = jnp.stack([lax.axis_index("walk").astype(jnp.int32), q_index[0]])
    odd_freq = jnp.broadcast_to((2 * freq_index + 1).astype(jnp.float32)[:, None], (NF, V))
    return accumulate(place, odd_freq, walkers)[None]


def solution(mesh):
    return jax.shard_map(
        local,
        mesh=mesh,
        in_specs=(
            P("walk", "blk", None, None),
            P("walk", "blk", None),
            P("walk", "blk", None),
            P(),
            P("blk"),
        ),
        out_specs=P("blk", None, "walk", None),
        check_vma=False,
    )
```

time: 244 us -> 47.4 us (0.19)
  local copies, waits for them, and re-layouts: 68.3 us -> 0.98 us
  waiting for transfers between devices: 63.6 us -> 8.99 us
  other arithmetic: 34.7 us -> 2.13 us
  matrix products: 27.2 us -> 0 us
  starting transfers between devices: 35.1 us -> 8.63 us
  Pallas kernels: 0 us -> 18.7 us
  between operations: 14.4 us -> 0.67 us
  blocking collectives: 0 us -> 6.89 us
    reduce_scatter x1 -> x0, waiting for transfers between devices: 59.5 us -> none  [settle(): lax.psum_scatter(running[None], 'walk', scatter_dimension=2, tiled=True)]
    gather x12 -> x0, local copies, waits for them, and re-layouts: 35.6 us -> none  [the longest x4 15.3 us: walker_term(): jnp.take(right_side, shifted, axis=0)]
    reshape x4 -> x0, local copies, waits for them, and re-layouts: 29.2 us -> none  [green_product(): return (table * (1.0 / V)).reshape(2, row_count, col_count)]
    dot_general x12 -> x0, matrix products: 27.2 us -> none  [the longest x8 23.8 us: green_product(): lax.dot_general(left_side, right_side, (((1,), (1,)), ((), ())), preferre...]
    ppermute x9 -> x3, starting transfers between devices: 35.1 us -> 8.63 us  [shifted_owner(): lax.ppermute(value, 'blk', [((i + steps) % count, i) for i in range(count)])]
    pallas_call x0 -> x1, Pallas kernels: none -> 18.7 us  [accumulate(): pl.pallas_call(walker_kernel, out_shape=jax.ShapeDtypeStruct((2, ROWS, K)...]
    add x2 -> x0, other arithmetic: 10.4 us -> none  [the longest x1 9.75 us: local(): first_half + lax.psum_scatter(running[None], 'walk', scatter_dimension=2,...]
    another operation x4 -> x2, other arithmetic: 10.4 us -> 0.74 us  [walker_term(): return jnp.stack([real_term, imag_term])]
  transfers between devices with their start and end apart: 10 -> 3, of which waited for: 2 -> 2; matrix products, arithmetic and copies ran while one was open for 30% -> 2% of each run, Pallas kernels for 0% -> 0%
where the time goes in v1:
time: 47.4 us; the launch traced here: 47 us
  Pallas kernels  18.7 us (39%)
  waiting for transfers between devices  8.99 us (19%)
  starting transfers between devices  8.63 us (18%)
  blocking collectives  6.89 us (15%)
  other arithmetic  2.13 us (4%)
  local copies, waits for them, and re-layouts  0.98 us (2%)
  between operations  0.67 us (1%)
    pallas_call x1, Pallas kernels, accumulate(): pl.pallas_call(walker_kernel, out_shape=jax.ShapeDtypeStruct((2, ROWS, K)...  18.7 us
    ppermute x3, waiting for transfers between devices, shifted_owner(): lax.ppermute(value, 'blk', [((i + steps) % count, i) for i in range(count)])  8.99 us
    ppermute x3, starting transfers between devices, shifted_owner(): lax.ppermute(value, 'blk', [((i + steps) % count, i) for i in range(count)])  8.63 us
    all_gather x1, blocking collectives, local(): groups = lax.all_gather(packed, 'walk', axis=0)  6.89 us
  transfers between devices with their start and end apart: 3, of which 2 were waited for; matrix products, arithmetic and copies ran while one was open for 2% of the time, Pallas kernels for 0%

profile of v1, /device:TPU:1, one launch (start us, length us, event | category | flops | bytes accessed | tf_op | source)
XLA Modules:
  0.0 47.0 jit_solution(12744793744870838786)
XLA Ops:
  0.0 0.7 %convert_bitcast_fusion = bf16[1,128]{1,0:T(2,128)(2,1)S(1)} fusion(s32[1,1,128]{2,1,0:T(1,128)} %param.7), kind=kLoop, calls=%fused_computation.9 | loop fusion | flops 128 | bytes 768 | tf_op jit(solution)/shard_map/squeeze | solution.py:144
  0.7 0.7 %fusion = (bf16[1,128]{1,0:T(2,128)(2,1)S(1)}, bf16[1,128]{1,0:T(2,128)(2,1)S(1)}) fusion(s32[1,1,128]{2,1,0:T(1,128)} %param.6), kind=kLoop, calls=%fused_computation.6 | loop fusion | flops 2688 | bytes 1024 | tf_op jit(solution)/shard_map/convert.1
  1.3 0.9 %concatenate.9 = bf16[144,128]{1,0:T(8,128)(2,1)S(1)} concatenate(bf16[128,128]{1,0:T(8,128)(2,1)} %bitcast.27, bf16[1,128]{1,0:T(2,128)(2,1)S(1)} %get-tuple-element.6, bf16[1,128]{1,0:T(2,128)(2,1)S(1)} %get-tuple-element.5, bf16[1,128]{1,0:T(2,128)(2,1)S(1)} %convert_bitcast_fusion, bf16[13,128]{1,0:T(8,128)(2,1)S(1)} %broadcast_in_dim.13), dimensions={0} | concatenate | bytes 73728 | tf_op jit(solution)/shard_map/concatenate | solution.py:146
  2.2 6.9 %all-gather = bf16[576,128]{1,0:T(8,128)(2,1)S(1)} all-gather(bf16[144,128]{1,0:T(8,128)(2,1)S(1)} %concatenate.9), channel_id=2, replica_groups=mesh['blk'=32,'walk'=4] {'walk'}, dimensions={0}, use_global_device_ids=true | all-gather | bytes 184320 | tf_op jit(solution)/shard_map/all_gather | solution.py:147
  9.1 4.9 %collective-permute-start.2 = (bf16[4,144,128]{2,1,0:T(8,128)(2,1)S(1)}, bf16[4,144,128]{2,1,0:T(8,128)(2,1)S(1)}, u32[]{:S(2)}, u32[]{:S(2)}) collective-permute-start(bf16[4,144,128]{2,1,0:T(8,128)(2,1)S(1)} %bitcast.23), channel_id=1, source_target_pairs={{8,0},{12,4},{16,8},{20,12},{24,16},{28,20},{32,24},{36,28},{40,32... | collective-permute-start | bytes 442376 | tf_op jit(solution)/shard_map/ppermute | solution.py:140
  14.1 3.7 %collective-permute-start.1 = (bf16[4,144,128]{2,1,0:T(8,128)(2,1)S(1)}, bf16[4,144,128]{2,1,0:T(8,128)(2,1)S(1)}, u32[]{:S(2)}, u32[]{:S(2)}) collective-permute-start(bf16[4,144,128]{2,1,0:T(8,128)(2,1)S(1)} %bitcast.24), channel_id=1, source_target_pairs={{4,0},{8,4},{12,8},{16,12},{20,16},{24,20},{28,24},{32,28},{36,32}... | collective-permute-start | bytes 442376 | tf_op jit(solution)/shard_map/ppermute | solution.py:140
  17.8 0.0 collective-permute-start
  17.8 0.7 %add_convert_fusion = f32[24]{0:T(128)S(1)} fusion(s32[24]{0:T(128)} %param.8), kind=kLoop, calls=%fused_computation.10 | loop fusion | flops 72 | bytes 192 | tf_op jit(solution)/shard_map/convert_element_type | solution.py:150
  19.1 0.1 pad_add_fusion.place_ref
  19.2 0.0 collective-permute-done.2
  19.2 2.3 %collective-permute-done.1 = bf16[4,144,128]{2,1,0:T(8,128)(2,1)S(1)} collective-permute-done((bf16[4,144,128]{2,1,0:T(8,128)(2,1)S(1)}, bf16[4,144,128]{2,1,0:T(8,128)(2,1)S(1)}, u32[]{:S(2)}, u32[]{:S(2)}) %collective-permute-start.1) | collective-permute-done | bytes 147488 | tf_op jit(solution)/shard_map/ppermute | solution.py:140
  21.4 6.7 %collective-permute-done = bf16[4,144,128]{2,1,0:T(8,128)(2,1)S(1)} collective-permute-done((bf16[4,144,128]{2,1,0:T(8,128)(2,1)S(1)}, bf16[4,144,128]{2,1,0:T(8,128)(2,1)S(1)}, u32[]{:S(2)}, u32[]{:S(2)}) %collective-permute-start) | collective-permute-done | bytes 147488 | tf_op jit(solution)/shard_map/ppermute | solution.py:140
  28.1 0.1 pad_maximum_fusion.walkers_ref
  28.2 0.1 broadcast_in_dim.12.odd_freq_ref
  28.3 18.7 %shard_map.55 = f32[2,216,864]{2,1,0:T(8,128)} custom-call(s32[2]{0:T(128)S(1)} %pad_add_fusion.place_ref, f32[24,128]{1,0:T(8,128)S(1)} %broadcast_in_dim.12.odd_freq_ref, bf16[16,144,128]{2,1,0:T(8,128)(2,1)S(1)} %pad_maximum_fusion.walkers_ref), custom_call_target="tpu_custom_call" | custom-call | tf_op jit(solution)/shard_map/pallas_call | solution.py:121
  (1 shorter events, 0.0 us)
Async XLA Ops:
  9.1 10.0 %collective-permute-start.2 = (bf16[4,144,128]{2,1,0:T(8,128)(2,1)S(1)}, bf16[4,144,128]{2,1,0:T(8,128)(2,1)S(1)}, u32[]{:S(2)}, u32[]{:S(2)}) collective-permute-start(bf16[4,144,128]{2,1,0:T(8,128)(2,1)S(1)} %bitcast.23), channel_id=1, source_target_pairs={{8,0},{12,4},{16,8},{20,12},{24,16},{28,20},{32,24},{36,28},{40,32... | collective-permute-start | bytes 442376 | tf_op jit(solution)/shard_map/ppermute | solution.py:140
  14.1 7.3 %collective-permute-start.1 = (bf16[4,144,128]{2,1,0:T(8,128)(2,1)S(1)}, bf16[4,144,128]{2,1,0:T(8,128)(2,1)S(1)}, u32[]{:S(2)}, u32[]{:S(2)}) collective-permute-start(bf16[4,144,128]{2,1,0:T(8,128)(2,1)S(1)} %bitcast.24), channel_id=1, source_target_pairs={{4,0},{8,4},{12,8},{16,12},{20,16},{24,20},{28,24},{32,28},{36,32}... | collective-permute-start | bytes 442376 | tf_op jit(solution)/shard_map/ppermute | solution.py:140
  17.8 10.4 %collective-permute-start = (bf16[4,144,128]{2,1,0:T(8,128)(2,1)S(1)}, bf16[4,144,128]{2,1,0:T(8,128)(2,1)S(1)}, u32[]{:S(2)}, u32[]{:S(2)}) collective-permute-start(bf16[4,144,128]{2,1,0:T(8,128)(2,1)S(1)} %bitcast.25), channel_id=1, source_target_pairs={{124,0},{0,4},{4,8},{8,12},{12,16},{16,20},{20,24},{24,28},{28,32}... | collective-permute-start | bytes 442376 | tf_op jit(solution)/shard_map/ppermute | solution.py:140

commit v2 on v1

v2 whole, which is shorter than its diff:
```python
import jax
import jax.numpy as jnp
from jax import lax
from jax.experimental import pallas as pl
from jax.experimental.pallas import tpu as pltpu
from jax.sharding import Mesh
from jax.sharding import PartitionSpec as P

SIDE = 6
NF = 24
K = 864
V = 128
STEPS = 4
ROWS = 216
PACK = 136
BLOCKS = 9
COL_TILES = ((0, 256), (256, 256), (512, 256), (768, 96))


def quarter_cos_sin(turns):
    near = jnp.floor(turns + 0.5)
    x = turns - near
    x2 = x * x
    s = x * (1.5707963267948966 + x2 * (-0.6459640975062462 + x2 * (0.07969262624616704 + x2 * (-0.004681754135318688 + x2 * 0.00016044118478735982))))
    c = 1.0 + x2 * (-1.2337005501361697 + x2 * (0.253669507901048 + x2 * (-0.02086348076335296 + x2 * (0.0009192602748394266 + x2 * -2.520204237306061e-05))))
    quad = near - 4.0 * jnp.floor(near * 0.25)
    odd = (quad == 1.0) | (quad == 3.0)
    cc = jnp.where(odd, s, c)
    ss = jnp.where(odd, c, s)
    cc = jnp.where((quad == 1.0) | (quad == 2.0), -cc, cc)
    ss = jnp.where(quad >= 2.0, -ss, ss)
    return cc, ss


def sixth_cos_sin(m):
    y = m - 6.0 * jnp.floor((m + 0.5) * (1.0 / 6.0))
    z = jnp.abs(y - 3.0)
    half = 0.8660254037844386
    c = jnp.where(z == 3.0, 1.0, jnp.where(z == 2.0, 0.5, jnp.where(z == 1.0, -0.5, -1.0)))
    s = jnp.where((z == 3.0) | (z == 0.0), 0.0, jnp.where(y < 3.0, half, -half))
    return c, s


def pieces(share, transfer, odd_freq_ref, walkers_ref, w, table_ref, left_ref):
    st = {}

    def rotated(c, s, row):
        c, s = c[row : row + 1], s[row : row + 1]
        fc, fs = st["f"]
        return fc * c + fs * s, fs * c - fc * s

    def stacked(c, s):
        blocks = [rotated(c, s, j) for j in range(BLOCKS)]
        return jnp.concatenate([b[0] for b in blocks] + [b[1] for b in blocks], axis=0).astype(jnp.bfloat16)

    def interleave(parts):
        return jnp.stack([p.reshape(27, 8, V) for p in parts], axis=1).reshape(K, V).astype(jnp.bfloat16)

    def p0():
        meta = walkers_ref[w, V:, :].astype(jnp.float32)
        times = meta[0:1] * 32.0 + meta[1:2]
        sites = meta[2:3]
        site_x = jnp.floor((sites + 0.5) * (1.0 / SIDE))
        site_y = sites - SIDE * site_x
        product = odd_freq_ref[...] * times
        st["f"] = quarter_cos_sin((product - 2048.0 * jnp.floor(product * (1.0 / 2048.0))) * (1.0 / 512.0))

        def rows_of(kx, ky):
            return sixth_cos_sin(kx * site_x + ky * site_y)

        index = lax.broadcasted_iota(jnp.int32, (16, V), 0)
        st["base"] = rows_of((index // 3).astype(jnp.float32), (index % 3).astype(jnp.float32))
        mine = index + BLOCKS * share
        mine_x = (mine // SIDE).astype(jnp.float32)
        mine_y = (mine % SIDE).astype(jnp.float32)
        q_x = (transfer // SIDE).astype(jnp.float32)
        q_y = (transfer % SIDE).astype(jnp.float32)
        moved = rows_of(mine_x + q_x, mine_y + q_y)
        mine = rows_of(mine_x, mine_y)
        turn_c, turn_s = rows_of(q_x, q_y)
        st["turn"] = turn_c[0:1] * (2.0 ** -18), turn_s[0:1] * (2.0 ** -18)
        st["flip_x"] = 1.0 - 2.0 * (site_x - 2.0 * jnp.floor(site_x * 0.5))
        st["flip_y"] = 1.0 - 2.0 * (site_y - 2.0 * jnp.floor(site_y * 0.5))
        matrix = walkers_ref[w, :V, :]
        st["first"] = jnp.dot(stacked(*moved), matrix, preferred_element_type=jnp.float32)
        st["second"] = lax.dot_general(stacked(*mine), matrix, (((1,), (1,)), ((), ())), preferred_element_type=jnp.float32)

    def p1():
        base_c, base_s = st["base"]
        flip_x, flip_y = st["flip_x"], st["flip_y"]
        for kx in range(3):
            blocks = [rotated(base_c, base_s, 3 * kx + ky) for ky in range(3)]
            blocks = blocks + [(c * flip_y, s * flip_y) for c, s in blocks]
            cos_part = jnp.concatenate([b[0] for b in blocks], axis=0).astype(jnp.bfloat16)
            sin_part = jnp.concatenate([b[1] for b in blocks], axis=0).astype(jnp.bfloat16)
            flip = flip_x.astype(jnp.bfloat16)
            table_ref[pl.ds(144 * kx, 144), 0:V] = cos_part
            table_ref[pl.ds(144 * kx, 144), V:] = sin_part
            table_ref[pl.ds(144 * (kx + 3), 144), 0:V] = cos_part * flip
            table_ref[pl.ds(144 * (kx + 3), 144), V:] = sin_part * flip

    def p2():
        first = st["first"]
        a_re, a_im = first[:ROWS], first[ROWS:]
        turn_c, turn_s = st["turn"]
        st["a"] = a_re * turn_c - a_im * turn_s, a_re * turn_s + a_im * turn_c
        second = st["second"]
        a_re, a_im = st["a"]
        b_re, b_im = second[:ROWS], second[ROWS:]
        left_ref[:, 0:V] = interleave([a_re, a_im, b_re, -b_im])
        left_ref[:, V:] = interleave([a_im, -a_re, b_im, b_re])

    return [p0, p1, p2]


def tile_main(t, table_ref, left_ref, acc_ref):
    start, size = COL_TILES[t]
    product = lax.dot_general(left_ref[...], table_ref[pl.ds(start, size), :], (((1,), (1,)), ((), ())), preferred_element_type=jnp.float32)
    product = product.reshape(27, 4, 8, size)
    m_re, m_im, n_re, n_im = (product[:, i] for i in range(4))
    acc_ref[0, :, pl.ds(start, size)] += (m_re * n_re - m_im * n_im).reshape(ROWS, size)
    acc_ref[1, :, pl.ds(start, size)] += (m_re * n_im + m_im * n_re).reshape(ROWS, size)


def pack_kernel(freq_hbm, matrix_hbm, times_hbm, labels_hbm, packed_ref, odd_freq_ref, freq_ref, times_ref, labels_ref, sem):
    copies = (
        pltpu.make_async_copy(matrix_hbm.at[0], packed_ref.at[:, pl.ds(0, V), :], sem.at[0]),
        pltpu.make_async_copy(times_hbm, times_ref, sem.at[1]),
        pltpu.make_async_copy(labels_hbm, labels_ref, sem.at[2]),
        pltpu.make_async_copy(freq_hbm, freq_ref, sem.at[3]),
    )
    for copy in copies:
        copy.start()
    for copy in copies[1:]:
        copy.wait()
    row = lax.broadcasted_iota(jnp.int32, (PACK - V, V), 0)
    times = jnp.broadcast_to(times_ref[0], (PACK - V, V))
    labels = jnp.broadcast_to(labels_ref[0], (PACK - V, V))
    meta = jnp.where(row == 0, times // 32, jnp.where(row == 1, times % 32, jnp.where(row == 2, labels, 0)))
    packed_ref[0, V:, :] = meta.astype(jnp.float32).astype(jnp.bfloat16)
    row = lax.broadcasted_iota(jnp.int32, (NF, V), 0)
    odd = jnp.zeros((NF, V), jnp.int32)
    for f in range(NF):
        odd = jnp.where(row == f, 2 * freq_ref[f] + 1, odd)
    odd_freq_ref[...] = odd.astype(jnp.float32)
    copies[0].wait()


def pack(freq_index, matrix, times, labels):
    vmem = pl.BlockSpec(memory_space=pltpu.VMEM)
    return pl.pallas_call(
        pack_kernel,
        out_shape=(
            jax.ShapeDtypeStruct((1, PACK, V), jnp.bfloat16),
            jax.ShapeDtypeStruct((NF, V), jnp.float32),
        ),
        in_specs=[pl.BlockSpec(memory_space=pl.ANY)] * 4,
        out_specs=(vmem, vmem),
        scratch_shapes=[
            pltpu.SMEM((NF,), jnp.int32),
            pltpu.VMEM((1, 1, V), jnp.int32),
            pltpu.VMEM((1, 1, V), jnp.int32),
            pltpu.SemaphoreType.DMA((4,)),
        ],
        compiler_params=pltpu.CompilerParams(vmem_limit_bytes=4 << 20),
        name="pack",
    )(*(pltpu.with_memory_space_constraint(x, pltpu.HBM) for x in (freq_index, matrix, times, labels)))


def absorb_kernel(first, final, share_ref, transfer_ref, odd_freq_ref, walkers_ref, *refs):
    if first:
        acc_ref, *refs = refs
    else:
        old_ref, acc_ref, *refs = refs
    if final:
        out_ref, *refs = refs
    table_a, left_a, table_b, left_b, sem = refs
    n = walkers_ref.shape[0]
    place = share_ref[0], transfer_ref[0], odd_freq_ref, walkers_ref
    if first:
        acc_ref[...] = jnp.zeros_like(acc_ref)
    for piece in pieces(*place, 0, table_a, left_a):
        piece()

    def copy(tile):
        cols = pl.ds(*COL_TILES[tile])
        return pltpu.make_async_copy(acc_ref.at[:, :, cols], out_ref.at[:, :, cols], sem.at[tile])

    def half(current, following, following_walker, last=False):
        todo = [] if following is None else pieces(*place, following_walker, *following)
        for tile in range(4):
            tile_main(tile, *current, acc_ref)
            if last:
                copy(tile).start()
            if tile < len(todo):
                todo[tile]()

    slot_a, slot_b = (table_a, left_a), (table_b, left_b)

    def body(i, carry):
        half(slot_a, slot_b, 2 * i + 1)
        half(slot_b, slot_a, 2 * i + 2)
        return carry

    if n > 2:
        lax.fori_loop(0, n // 2 - 1, body, 0)
    half(slot_a, slot_b, n - 1)
    half(slot_b, None, None, last=final)
    if final:
        for tile in range(4):
            copy(tile).wait()


def absorb(share, transfer, odd_freq, walkers, acc=None, final=False):
    n = walkers.shape[0]
    vmem = pl.BlockSpec(memory_space=pltpu.VMEM)
    smem = pl.BlockSpec(memory_space=pltpu.SMEM)
    total = jax.ShapeDtypeStruct((2, ROWS, K), jnp.float32)
    args = [share, transfer, odd_freq, walkers] + ([] if acc is None else [acc])
    result = pl.pallas_call(
        lambda *refs: absorb_kernel(acc is None, final, *refs),
        out_shape=(total, total) if final else (total,),
        in_specs=[smem, smem] + [vmem] * (len(args) - 2),
        out_specs=(vmem, pl.BlockSpec(memory_space=pl.ANY)) if final else (vmem,),
        scratch_shapes=[pltpu.VMEM((K, 256), jnp.bfloat16)] * 4 + [pltpu.SemaphoreType.DMA((4,))],
        input_output_aliases={} if acc is None else {4: 0},
        cost_estimate=pl.CostEstimate(flops=n * 450_000_000, bytes_accessed=n * 40_000, transcendentals=0),
        compiler_params=pltpu.CompilerParams(vmem_limit_bytes=16 << 20),
        name="absorb",
    )(*args)
    return result[-1]


COORDS = ("x", "y", "zh", "zl", "core")


def permute(value, source):
    pairs = []
    for target in range(128):
        x, y, zh, zl, core = target // 32, target // 8 % 4, target // 4 % 2, target // 2 % 2, target % 2
        place = source(x, y, zh, zl, core)
        if place is not None:
            x, y, zh, zl, core = place
            pairs.append(((((x * 4 + y) * 2 + zh) * 2 + zl) * 2 + core, target))
    return lax.ppermute(value, COORDS, pairs)


def owner_at(steps):
    def source(x, y, zh, zl, core):
        owner = ((x * 4 + y) * 2 + zh + steps) % 32
        return owner // 8, owner // 2 % 4, owner % 2, zl, core

    return source


def local(walker_m, vertex_times, vertex_labels, freq_index, q_index):
    own, odd_freq = pack(freq_index, walker_m, vertex_times, vertex_labels)
    share = (2 * lax.axis_index("zl") + lax.axis_index("core")).astype(jnp.int32).reshape(1)
    ahead = permute(own, owner_at(2))
    behind = permute(own, lambda x, y, zh, zl, core: owner_at(-2)(x, y, zh, zl, core) if zh == 1 else None)
    odd_owner = lax.axis_index("zh") == 1
    send = jnp.concatenate([own, jnp.where(odd_owner, behind, ahead)], axis=0)
    other = permute(send, lambda x, y, zh, zl, core: (x, y, 1 - zh, zl, core))
    group = jnp.concatenate([own, ahead, other], axis=0)
    near = permute(group, lambda x, y, zh, zl, core: (x, y, zh, 1 - zl, core))
    acc = absorb(share, q_index, odd_freq, group)
    near, acc = lax.optimization_barrier((near, acc))
    far = permute(jnp.concatenate([group, near], axis=0), lambda x, y, zh, zl, core: (x, y, zh, zl, 1 - core))
    acc = absorb(share, q_index, odd_freq, near, acc)
    out = absorb(share, q_index, odd_freq, far, acc, final=True)
    return out[None]


def solution(mesh):
    fine = Mesh(mesh.devices.reshape(4, 4, 2, 2, 2), COORDS)
    walk, blk = ("zl", "core"), ("x", "y", "zh")
    return jax.shard_map(
        local,
        mesh=fine,
        in_specs=(P(walk, blk, None, None), P(walk, blk, None), P(walk, blk, None), P(), P(blk)),
        out_specs=P(blk, None, walk, None),
        check_vma=False,
    )
```

time: 47.4 us -> 33.4 us (0.70)
  starting transfers between devices: 8.63 us -> 15.8 us
  blocking collectives: 6.89 us -> 0 us
  waiting for transfers between devices: 8.99 us -> 2.6 us
  Pallas kernels: 18.7 us -> 14 us
  other arithmetic: 2.13 us -> 0.06 us
  local copies, waits for them, and re-layouts: 0.98 us -> 0.02 us
    ppermute x3 -> x5, starting transfers between devices: 8.63 us -> 15.8 us  [permute(): return lax.ppermute(value, COORDS, pairs)]
    all_gather x1 -> x0, blocking collectives: 6.89 us -> none  [local(): groups = lax.all_gather(packed, 'walk', axis=0)]
    ppermute x3 -> x5, waiting for transfers between devices: 8.99 us -> 2.6 us  [permute(): return lax.ppermute(value, COORDS, pairs)]
    pallas_call x1 -> x4, Pallas kernels: 18.7 us -> 14 us  [the longest x3 13.2 us: absorb(): pl.pallas_call(lambda *refs: absorb_kernel(acc is None, final, *refs), ou...]
    concatenate x1, local copies, waits for them, and re-layouts: 0.91 us -> 0.01 us  [local(): group = jnp.concatenate([own, ahead, other], axis=0)]
    another operation x2 -> x0, other arithmetic: 0.74 us -> none
    convert_element_type x1 -> x0, other arithmetic: 0.66 us -> none  [local(): (2 * freq_index + 1).astype(jnp.float32)[:, None]]
    squeeze x1 -> x0, other arithmetic: 0.66 us -> none  [local(): times, labels = (vertex_times[0], vertex_labels[0])]
  transfers between devices with their start and end apart: 3 -> 5, of which waited for: 2 -> 3; matrix products, arithmetic and copies ran while one was open for 2% -> 0% of each run, Pallas kernels for 0% -> 18%
where the time goes in v2:
time: 33.4 us; the launch traced here: 33.3 us
  starting transfers between devices  15.8 us (47%)
  Pallas kernels  14 us (42%)
  waiting for transfers between devices  2.6 us (8%)
  between operations  0.71 us (2%)
    ppermute x5, starting transfers between devices, permute(): return lax.ppermute(value, COORDS, pairs)  15.8 us
    pallas_call x3, Pallas kernels, absorb(): pl.pallas_call(lambda *refs: absorb_kernel(acc is None, final, *refs), ou...  13.2 us
    ppermute x5, waiting for transfers between devices, permute(): return lax.ppermute(value, COORDS, pairs)  2.6 us
    pallas_call x1, Pallas kernels, pack(): pl.pallas_call(pack_kernel, out_shape=(jax.ShapeDtypeStruct((1, PACK, V),...  0.86 us
  transfers between devices with their start and end apart: 5, of which 3 were waited for; matrix products, arithmetic and copies ran while one was open for 0% of the time, Pallas kernels for 18%

profile of v2, /device:TPU:1, one launch (start us, length us, event | category | flops | bytes accessed | tf_op | source)
XLA Modules:
  0.0 33.3 jit_solution(13790917612629247412)
XLA Ops:
  0.0 0.9 %pack.1 = (bf16[1,136,128]{2,1,0:T(8,128)(2,1)S(1)}, f32[24,128]{1,0:T(8,128)S(1)}) custom-call(s32[24]{0:T(128)} %freq_hbm.1, bf16[1,1,128,128]{3,2,1,0:T(8,128)(2,1)} %matrix_hbm.1, s32[1,1,128]{2,1,0:T(1,128)} %times_hbm.1, s32[1,1,128]{2,1,0:T(1,128)} %labels_hbm.1), custom_call_target="tpu_custom_call" | custom-call | tf_op jit(solution)/shard_map/pack/pallas_call | solution.py:151
  0.9 0.7 %collective-permute-start.1 = (bf16[1,136,128]{2,1,0:T(8,128)(2,1)S(1)}, bf16[1,136,128]{2,1,0:T(8,128)(2,1)S(1)}, u32[]{:S(2)}, u32[]{:S(2)}) collective-permute-start(bf16[1,136,128]{2,1,0:T(8,128)(2,1)S(1)} %get-tuple-element.11), channel_id=1, source_target_pairs={{124,4},{125,5},{126,6},{127,7},{4,12},{5,13},{6,14},{7,15},{12,20... | collective-permute-start | bytes 104456 | tf_op jit(solution)/shard_map/ppermute | solution.py:245
  1.5 5.8 %collective-permute-start = (bf16[1,136,128]{2,1,0:T(8,128)(2,1)S(1)}, bf16[1,136,128]{2,1,0:T(8,128)(2,1)S(1)}, u32[]{:S(2)}, u32[]{:S(2)}) collective-permute-start(bf16[1,136,128]{2,1,0:T(8,128)(2,1)S(1)} %get-tuple-element.11), channel_id=1, source_target_pairs={{8,0},{9,1},{10,2},{11,3},{12,4},{13,5},{14,6},{15,7},{16,8},{17,9... | collective-permute-start | bytes 104456 | tf_op jit(solution)/shard_map/ppermute | solution.py:245
  7.4 0.0 collective-permute-done.1
  7.4 1.0 %collective-permute-done = bf16[1,136,128]{2,1,0:T(8,128)(2,1)S(1)} collective-permute-done((bf16[1,136,128]{2,1,0:T(8,128)(2,1)S(1)}, bf16[1,136,128]{2,1,0:T(8,128)(2,1)S(1)}, u32[]{:S(2)}, u32[]{:S(2)}) %collective-permute-start) | collective-permute-done | bytes 34848 | tf_op jit(solution)/shard_map/ppermute | solution.py:245
  8.4 5.1 %collective-permute-start.2 = (bf16[2,136,128]{2,1,0:T(8,128)(2,1)S(1)}, bf16[2,136,128]{2,1,0:T(8,128)(2,1)S(1)}, u32[]{:S(2)}, u32[]{:S(2)}) collective-permute-start(bf16[2,136,128]{2,1,0:T(8,128)(2,1)S(1)} %pad_maximum_fusion.1), channel_id=1, source_target_pairs={{4,0},{5,1},{6,2},{7,3},{0,4},{1,5},{2,6},{3,7},{12,8},{13,9},{14,... | collective-permute-start | bytes 208904 | tf_op jit(solution)/shard_map/ppermute | solution.py:245
  14.2 1.0 %collective-permute-done.2 = bf16[2,136,128]{2,1,0:T(8,128)(2,1)S(1)} collective-permute-done((bf16[2,136,128]{2,1,0:T(8,128)(2,1)S(1)}, bf16[2,136,128]{2,1,0:T(8,128)(2,1)S(1)}, u32[]{:S(2)}, u32[]{:S(2)}) %collective-permute-start.2) | collective-permute-done | bytes 69664 | tf_op jit(solution)/shard_map/ppermute | solution.py:245
  15.3 0.8 %collective-permute-start.3 = (bf16[4,136,128]{2,1,0:T(8,128)(2,1)S(1)}, bf16[4,136,128]{2,1,0:T(8,128)(2,1)S(1)}, u32[]{:S(2)}, u32[]{:S(2)}) collective-permute-start(bf16[4,136,128]{2,1,0:T(8,128)(2,1)S(1)} %constant_dynamic-update-slice_fusion.refs_3_), channel_id=1, source_target_pairs={{2,0},{3,1},{0,2},{1,3},{6,4},{7,5},{4,6},{5,7},{10,8},{11,9},{8,1... | collective-permute-start | bytes 417800 | tf_op jit(solution)/shard_map/ppermute | solution.py:245
  16.1 3.0 %absorb.3.refs_4_ = f32[2,216,864]{2,1,0:T(8,128)S(1)} custom-call(s32[1]{0:T(128)} %bitcast.refs_0_, s32[1]{0:T(128)S(6)} %copy.12.refs_1_, f32[24,128]{1,0:T(8,128)S(1)} %get-tuple-element.10.refs_2_, bf16[4,136,128]{2,1,0:T(8,128)(2,1)S(1)} %constant_dynamic-update-slice_fusion.refs_3_), custom_call_target="tpu_custom_call" | custom-call | flops 1800000000 | bytes 160000 | tf_op jit(solution)/shard_map/absorb/pallas_call | solution.py:220
  19.1 0.5 %collective-permute-done.3.refs_3_ = bf16[4,136,128]{2,1,0:T(8,128)(2,1)S(1)} collective-permute-done((bf16[4,136,128]{2,1,0:T(8,128)(2,1)S(1)}, bf16[4,136,128]{2,1,0:T(8,128)(2,1)S(1)}, u32[]{:S(2)}, u32[]{:S(2)}) %collective-permute-start.3) | collective-permute-done | bytes 139296 | tf_op jit(solution)/shard_map/ppermute | solution.py:245
  19.7 3.4 %collective-permute-start.4 = (bf16[8,136,128]{2,1,0:T(8,128)(2,1)S(1)}, bf16[8,136,128]{2,1,0:T(8,128)(2,1)S(1)}, u32[]{:S(2)}, u32[]{:S(2)}) collective-permute-start(bf16[8,136,128]{2,1,0:T(8,128)(2,1)S(1)} %pad_maximum_fusion), channel_id=1, source_target_pairs={{1,0},{0,1},{3,2},{2,3},{5,4},{4,5},{7,6},{6,7},{9,8},{8,9},{11,10... | collective-permute-start | bytes 835592 | tf_op jit(solution)/shard_map/ppermute | solution.py:245
  23.1 3.0 %absorb.4.refs_4_ = f32[2,216,864]{2,1,0:T(8,128)S(1)} custom-call(s32[1]{0:T(128)} %bitcast.refs_0_, s32[1]{0:T(128)S(6)} %copy.12.refs_1_, f32[24,128]{1,0:T(8,128)S(1)} %get-tuple-element.10.refs_2_, bf16[4,136,128]{2,1,0:T(8,128)(2,1)S(1)} %collective-permute-done.3.refs_3_, f32[2,216,864]{2,1,0:T(8,128)S(1)} %absorb.3.refs_4_), custom_call_target="tpu_custom_call", output_to_operand_aliasing={{}: (4, {})} | custom-call | flops 1800000000 | bytes 160000 | tf_op jit(solution)/shard_map/absorb/pallas_call | solution.py:220
  26.1 0.0 collective-permute-done.4.refs_3_
  26.1 7.1 %absorb.5 = (f32[2,216,864]{2,1,0:T(8,128)S(1)}, f32[2,216,864]{2,1,0:T(8,128)}) custom-call(s32[1]{0:T(128)} %bitcast.refs_0_, s32[1]{0:T(128)S(6)} %copy.12.refs_1_, f32[24,128]{1,0:T(8,128)S(1)} %get-tuple-element.10.refs_2_, bf16[8,136,128]{2,1,0:T(8,128)(2,1)S(1)} %collective-permute-done.4.refs_3_, ...), custom_call_target="tpu_custom_call", output_to_operand_aliasing={{0}: (4, {})} | custom-call | flops 3600000000 | bytes 320000 | tf_op jit(solution)/shard_map/absorb/pallas_call | solution.py:220
  (5 shorter events, 0.1 us)
Async XLA Ops:
  0.9 6.5 %collective-permute-start.1 = (bf16[1,136,128]{2,1,0:T(8,128)(2,1)S(1)}, bf16[1,136,128]{2,1,0:T(8,128)(2,1)S(1)}, u32[]{:S(2)}, u32[]{:S(2)}) collective-permute-start(bf16[1,136,128]{2,1,0:T(8,128)(2,1)S(1)} %get-tuple-element.11), channel_id=1, source_target_pairs={{124,4},{125,5},{126,6},{127,7},{4,12},{5,13},{6,14},{7,15},{12,20... | collective-permute-start | bytes 104456 | tf_op jit(solution)/shard_map/ppermute | solution.py:245
  1.5 6.9 %collective-permute-start = (bf16[1,136,128]{2,1,0:T(8,128)(2,1)S(1)}, bf16[1,136,128]{2,1,0:T(8,128)(2,1)S(1)}, u32[]{:S(2)}, u32[]{:S(2)}) collective-permute-start(bf16[1,136,128]{2,1,0:T(8,128)(2,1)S(1)} %get-tuple-element.11), channel_id=1, source_target_pairs={{8,0},{9,1},{10,2},{11,3},{12,4},{13,5},{14,6},{15,7},{16,8},{17,9... | collective-permute-start | bytes 104456 | tf_op jit(solution)/shard_map/ppermute | solution.py:245
  8.4 6.8 %collective-permute-start.2 = (bf16[2,136,128]{2,1,0:T(8,128)(2,1)S(1)}, bf16[2,136,128]{2,1,0:T(8,128)(2,1)S(1)}, u32[]{:S(2)}, u32[]{:S(2)}) collective-permute-start(bf16[2,136,128]{2,1,0:T(8,128)(2,1)S(1)} %pad_maximum_fusion.1), channel_id=1, source_target_pairs={{4,0},{5,1},{6,2},{7,3},{0,4},{1,5},{2,6},{3,7},{12,8},{13,9},{14,... | collective-permute-start | bytes 208904 | tf_op jit(solution)/shard_map/ppermute | solution.py:245
  15.3 4.3 %collective-permute-start.3 = (bf16[4,136,128]{2,1,0:T(8,128)(2,1)S(1)}, bf16[4,136,128]{2,1,0:T(8,128)(2,1)S(1)}, u32[]{:S(2)}, u32[]{:S(2)}) collective-permute-start(bf16[4,136,128]{2,1,0:T(8,128)(2,1)S(1)} %constant_dynamic-update-slice_fusion.refs_3_), channel_id=1, source_target_pairs={{2,0},{3,1},{0,2},{1,3},{6,4},{7,5},{4,6},{5,7},{10,8},{11,9},{8,1... | collective-permute-start | bytes 417800 | tf_op jit(solution)/shard_map/ppermute | solution.py:245
  19.7 6.5 %collective-permute-start.4 = (bf16[8,136,128]{2,1,0:T(8,128)(2,1)S(1)}, bf16[8,136,128]{2,1,0:T(8,128)(2,1)S(1)}, u32[]{:S(2)}, u32[]{:S(2)}) collective-permute-start(bf16[8,136,128]{2,1,0:T(8,128)(2,1)S(1)} %pad_maximum_fusion), channel_id=1, source_target_pairs={{1,0},{0,1},{3,2},{2,3},{5,4},{4,5},{7,6},{6,7},{9,8},{8,9},{11,10... | collective-permute-start | bytes 835592 | tf_op jit(solution)/shard_map/ppermute | solution.py:245

commit v3 on v2

--- a/solution.py
+++ b/solution.py
@@ -167,48 +167,53 @@
     )(*(pltpu.with_memory_space_constraint(x, pltpu.HBM) for x in (freq_index, matrix, times, labels)))
 
 
-def absorb_kernel(first, final, share_ref, transfer_ref, odd_freq_ref, walkers_ref, *refs):
+def absorb_kernel(first, share_ref, transfer_ref, odd_freq_ref, walkers_ref, *refs):
     if first:
-        acc_ref, *refs = refs
+        acc_ref, *slots = refs
+        acc_ref[...] = jnp.zeros_like(acc_ref)
     else:
-        old_ref, acc_ref, *refs = refs
-    if final:
-        out_ref, *refs = refs
-    table_a, left_a, table_b, left_b, sem = refs
+        old_ref, acc_ref, *slots = refs
     n = walkers_ref.shape[0]
     place = share_ref[0], transfer_ref[0], odd_freq_ref, walkers_ref
-    if first:
-        acc_ref[...] = jnp.zeros_like(acc_ref)
-    for piece in pieces(*place, 0, table_a, left_a):
+    slots = slots[0:2], slots[2:4]
+    for piece in pieces(*place, 0, *slots[0]):
         piece()
+    for w in range(n):
+        todo = pieces(*place, w + 1, *slots[(w + 1) % 2]) if w + 1 < n else []
+        for tile in range(4):
+            tile_main(tile, *slots[w % 2], acc_ref)
+            if tile < len(todo):
+                todo[tile]()
+
+
+def finish_kernel(share_ref, transfer_ref, odd_freq_ref, walkers_ref, old_ref, acc_ref, out_ref, *refs):
+    n = walkers_ref.shape[0]
+    place = share_ref[0], transfer_ref[0], odd_freq_ref, walkers_ref
+    slots = [refs[2 * w : 2 * w + 2] for w in range(n)]
+    sem = refs[2 * n]
 
     def copy(tile):
         cols = pl.ds(*COL_TILES[tile])
         return pltpu.make_async_copy(acc_ref.at[:, :, cols], out_ref.at[:, :, cols], sem.at[tile])
 
-    def half(current, following, following_walker, last=False):
-        todo = [] if following is None else pieces(*place, following_walker, *following)
-        for tile in range(4):
-            tile_main(tile, *current, acc_ref)
-            if last:
-                copy(tile).start()
-            if tile < len(todo):
-                todo[tile]()
-
-    slot_a, slot_b = (table_a, left_a), (table_b, left_b)
-
-    def body(i, carry):
-        half(slot_a, slot_b, 2 * i + 1)
-        half(slot_b, slot_a, 2 * i + 2)
-        return carry
-
-    if n > 2:
-        lax.fori_loop(0, n // 2 - 1, body, 0)
-    half(slot_a, slot_b, n - 1)
-    half(slot_b, None, None, last=final)
-    if final:
-        for tile in range(4):
-            copy(tile).wait()
+    for piece in pieces(*place, 0, *slots[0]):
+        piece()
+    for w in range(n):
+        todo = pieces(*place, w + 1, *slots[w + 1]) if w + 1 < n else [lambda: None] * 3
+        todo[0]()
+        tile_main(0, *slots[w], acc_ref)
+        todo[1]()
+        if w + 1 == n:
+            copy(0).start()
+        tile_main(1, *slots[w], acc_ref)
+        todo[2]()
+    copy(1).start()
+    for tile in (2, 3):
+        for w in range(n):
+            tile_main(tile, *slots[w], acc_ref)
+        copy(tile).start()
+    for tile in range(4):
+        copy(tile).wait()
 
 
 def absorb(share, transfer, odd_freq, walkers, acc=None, final=False):
@@ -217,16 +222,17 @@
     smem = pl.BlockSpec(memory_space=pltpu.SMEM)
     total = jax.ShapeDtypeStruct((2, ROWS, K), jnp.float32)
     args = [share, transfer, odd_freq, walkers] + ([] if acc is None else [acc])
+    slots = n if final else 2
     result = pl.pallas_call(
-        lambda *refs: absorb_kernel(acc is None, final, *refs),
+        finish_kernel if final else lambda *refs: absorb_kernel(acc is None, *refs),
         out_shape=(total, total) if final else (total,),
         in_specs=[smem, smem] + [vmem] * (len(args) - 2),
         out_specs=(vmem, pl.BlockSpec(memory_space=pl.ANY)) if final else (vmem,),
-        scratch_shapes=[pltpu.VMEM((K, 256), jnp.bfloat16)] * 4 + [pltpu.SemaphoreType.DMA((4,))],
+        scratch_shapes=[pltpu.VMEM((K, 256), jnp.bfloat16)] * (2 * slots) + [pltpu.SemaphoreType.DMA((4,))] * final,
         input_output_aliases={} if acc is None else {4: 0},
         cost_estimate=pl.CostEstimate(flops=n * 450_000_000, bytes_accessed=n * 40_000, transcendentals=0),
         compiler_params=pltpu.CompilerParams(vmem_limit_bytes=16 << 20),
-        name="absorb",
+        name="finish" if final else "absorb",
     )(*args)
     return result[-1]
 
@@ -253,22 +259,37 @@
     return source
 
 
+def after(value, *others):
+    return lax.optimization_barrier((value, *others))
+
+
 def local(walker_m, vertex_times, vertex_labels, freq_index, q_index):
     own, odd_freq = pack(freq_index, walker_m, vertex_times, vertex_labels)
     share = (2 * lax.axis_index("zl") + lax.axis_index("core")).astype(jnp.int32).reshape(1)
+
+    def add(walkers, acc=None, final=False):
+        return absorb(share, q_index, odd_freq, walkers, acc, final)
+
+    behind = permute(own, owner_at(-2))
     ahead = permute(own, owner_at(2))
-    behind = permute(own, lambda x, y, zh, zl, core: owner_at(-2)(x, y, zh, zl, core) if zh == 1 else None)
+    acc = add(own)
+    ahead, behind, acc = after(ahead, behind, acc)
     odd_owner = lax.axis_index("zh") == 1
     send = jnp.concatenate([own, jnp.where(odd_owner, behind, ahead)], axis=0)
-    other = permute(send, lambda x, y, zh, zl, core: (x, y, 1 - zh, zl, core))
+    other = permute(send, lambda x, y, zh, zl, core: (x, y, 1 - zh, 1 - zl, core))
+    acc = add(ahead, acc)
+    other, acc = after(other, acc)
     group = jnp.concatenate([own, ahead, other], axis=0)
     near = permute(group, lambda x, y, zh, zl, core: (x, y, zh, 1 - zl, core))
-    acc = absorb(share, q_index, odd_freq, group)
-    near, acc = lax.optimization_barrier((near, acc))
-    far = permute(jnp.concatenate([group, near], axis=0), lambda x, y, zh, zl, core: (x, y, zh, zl, 1 - core))
-    acc = absorb(share, q_index, odd_freq, near, acc)
-    out = absorb(share, q_index, odd_freq, far, acc, final=True)
-    return out[None]
+    group_far = permute(group, lambda x, y, zh, zl, core: (x, y, zh, zl, 1 - core))
+    acc = add(other, acc)
+    group_far, acc = after(group_far, acc)
+    acc = add(group_far, acc)
+    near, acc = after(near, acc)
+    near_far = permute(near, lambda x, y, zh, zl, core: (x, y, zh, zl, 1 - core))
+    acc = add(near, acc)
+    near_far, acc = after(near_far, acc)
+    return add(near_far, acc, True)[None]
 
 
 def solution(mesh):

time: 33.4 us -> 29.3 us (0.88)
  starting transfers between devices: 15.8 us -> 12.9 us
  waiting for transfers between devices: 2.6 us -> 1.58 us
    ppermute x5 -> x6, starting transfers between devices: 15.8 us -> 12.9 us  [permute(): return lax.ppermute(value, COORDS, pairs)]
    ppermute x5 -> x6, waiting for transfers between devices: 2.6 us -> 1.58 us  [permute(): return lax.ppermute(value, COORDS, pairs)]
    pallas_call x3 -> x6, Pallas kernels: 13.2 us -> 12.9 us  [absorb(): pl.pallas_call(finish_kernel if final else lambda *refs: absorb_kernel(ac...]
  transfers between devices with their start and end apart: 5 -> 6, of which waited for: 3 -> 2; matrix products, arithmetic and copies ran while one was open for 0% -> 0% of each run, Pallas kernels for 18% -> 31%
where the time goes in v3:
time: 29.3 us; the launch traced here: 29.2 us
  Pallas kernels  13.7 us (47%)
  starting transfers between devices  12.9 us (44%)
  waiting for transfers between devices  1.58 us (5%)
  between operations  0.9 us (3%)
    ppermute x6, starting transfers between devices, permute(): return lax.ppermute(value, COORDS, pairs)  12.9 us
    pallas_call x6, Pallas kernels, absorb(): pl.pallas_call(finish_kernel if final else lambda *refs: absorb_kernel(ac...  12.9 us
    ppermute x6, waiting for transfers between devices, permute(): return lax.ppermute(value, COORDS, pairs)  1.58 us
    pallas_call x1, Pallas kernels, pack(): pl.pallas_call(pack_kernel, out_shape=(jax.ShapeDtypeStruct((1, PACK, V),...  0.86 us
  transfers between devices with their start and end apart: 6, of which 2 were waited for; matrix products, arithmetic and copies ran while one was open for 0% of the time, Pallas kernels for 31%

profile of v3, /device:TPU:1, one launch (start us, length us, event | category | flops | bytes accessed | tf_op | source)
XLA Modules:
  0.0 29.2 jit_solution(9544284573784571487)
XLA Ops:
  0.0 0.9 %pack.1 = (bf16[1,136,128]{2,1,0:T(8,128)(2,1)S(1)}, f32[24,128]{1,0:T(8,128)S(1)}) custom-call(s32[24]{0:T(128)} %freq_hbm.1, bf16[1,1,128,128]{3,2,1,0:T(8,128)(2,1)} %matrix_hbm.1, s32[1,1,128]{2,1,0:T(1,128)} %times_hbm.1, s32[1,1,128]{2,1,0:T(1,128)} %labels_hbm.1), custom_call_target="tpu_custom_call" | custom-call | tf_op jit(solution)/shard_map/pack/pallas_call | solution.py:151
  0.9 2.2 %collective-permute-start.1 = (bf16[1,136,128]{2,1,0:T(8,128)(2,1)S(1)}, bf16[1,136,128]{2,1,0:T(8,128)(2,1)S(1)}, u32[]{:S(2)}, u32[]{:S(2)}) collective-permute-start(bf16[1,136,128]{2,1,0:T(8,128)(2,1)S(1)} %get-tuple-element.20.refs_3_), channel_id=1, source_target_pairs={{120,0},{121,1},{122,2},{123,3},{124,4},{125,5},{126,6},{127,7},{0... | collective-permute-start | bytes 104456 | tf_op jit(solution)/shard_map/ppermute | solution.py:251
  3.1 3.7 %collective-permute-start = (bf16[1,136,128]{2,1,0:T(8,128)(2,1)S(1)}, bf16[1,136,128]{2,1,0:T(8,128)(2,1)S(1)}, u32[]{:S(2)}, u32[]{:S(2)}) collective-permute-start(bf16[1,136,128]{2,1,0:T(8,128)(2,1)S(1)} %get-tuple-element.20.refs_3_), channel_id=1, source_target_pairs={{8,0},{9,1},{10,2},{11,3},{12,4},{13,5},{14,6},{15,7},{16,8},{17,9... | collective-permute-start | bytes 104456 | tf_op jit(solution)/shard_map/ppermute | solution.py:251
  7.4 0.9 %absorb.5.refs_4_ = f32[2,216,864]{2,1,0:T(8,128)S(1)} custom-call(s32[1]{0:T(128)} %bitcast.refs_0_.share_ref, s32[1]{0:T(128)S(6)} %copy.18.refs_1_.transfer_ref, f32[24,128]{1,0:T(8,128)S(1)} %get-tuple-element.19.refs_2_.odd_freq_ref, bf16[1,136,128]{2,1,0:T(8,128)(2,1)S(1)} %get-tuple-element.20.refs_3_), custom_call_target="tpu_custom_call" | custom-call | flops 450000000 | bytes 40000 | tf_op jit(solution)/shard_map/absorb/pallas_call | solution.py:226
  8.3 0.0 collective-permute-done.1
  8.3 0.0 collective-permute-done.refs_3_
  8.4 3.8 %collective-permute-start.2 = (bf16[2,136,128]{2,1,0:T(8,128)(2,1)S(1)}, bf16[2,136,128]{2,1,0:T(8,128)(2,1)S(1)}, u32[]{:S(2)}, u32[]{:S(2)}) collective-permute-start(bf16[2,136,128]{2,1,0:T(8,128)(2,1)S(1)} %pad_maximum_fusion), channel_id=1, source_target_pairs={{6,0},{7,1},{4,2},{5,3},{2,4},{3,5},{0,6},{1,7},{14,8},{15,9},{12,... | collective-permute-start | bytes 208904 | tf_op jit(solution)/shard_map/ppermute | solution.py:251
  12.2 0.9 %absorb.6.refs_4_ = f32[2,216,864]{2,1,0:T(8,128)S(1)} custom-call(s32[1]{0:T(128)} %bitcast.refs_0_.share_ref, s32[1]{0:T(128)S(6)} %copy.18.refs_1_.transfer_ref, f32[24,128]{1,0:T(8,128)S(1)} %get-tuple-element.19.refs_2_.odd_freq_ref, bf16[1,136,128]{2,1,0:T(8,128)(2,1)S(1)} %collective-permute-done.refs_3_, ...), custom_call_target="tpu_custom_call", output_to_operand_aliasing={{}: (4, {})} | custom-call | flops 450000000 | bytes 40000 | tf_op jit(solution)/shard_map/absorb/pallas_call | solution.py:226
  13.1 0.8 %collective-permute-done.2.refs_3_ = bf16[2,136,128]{2,1,0:T(8,128)(2,1)S(1)} collective-permute-done((bf16[2,136,128]{2,1,0:T(8,128)(2,1)S(1)}, bf16[2,136,128]{2,1,0:T(8,128)(2,1)S(1)}, u32[]{:S(2)}, u32[]{:S(2)}) %collective-permute-start.2) | collective-permute-done | bytes 69664 | tf_op jit(solution)/shard_map/ppermute | solution.py:251
  13.9 2.3 %collective-permute-start.4 = (bf16[4,136,128]{2,1,0:T(8,128)(2,1)S(1)}, bf16[4,136,128]{2,1,0:T(8,128)(2,1)S(1)}, u32[]{:S(2)}, u32[]{:S(2)}) collective-permute-start(bf16[4,136,128]{2,1,0:T(8,128)(2,1)S(1)} %constant_dynamic-update-slice_fusion), channel_id=1, source_target_pairs={{1,0},{0,1},{3,2},{2,3},{5,4},{4,5},{7,6},{6,7},{9,8},{8,9},{11,10... | collective-permute-start | bytes 417800 | tf_op jit(solution)/shard_map/ppermute | solution.py:251
  16.2 0.0 collective-permute-start.3
  16.2 1.5 %absorb.7.refs_4_ = f32[2,216,864]{2,1,0:T(8,128)S(1)} custom-call(s32[1]{0:T(128)} %bitcast.refs_0_.share_ref, s32[1]{0:T(128)S(6)} %copy.18.refs_1_.transfer_ref, f32[24,128]{1,0:T(8,128)S(1)} %get-tuple-element.19.refs_2_.odd_freq_ref, bf16[2,136,128]{2,1,0:T(8,128)(2,1)S(1)} %collective-permute-done.2.refs_3_, ...), custom_call_target="tpu_custom_call", output_to_operand_aliasing={{}: (4, {})} | custom-call | flops 900000000 | bytes 80000 | tf_op jit(solution)/shard_map/absorb/pallas_call | solution.py:226
  17.8 0.0 collective-permute-done.4.refs_3_
  17.8 2.9 %absorb.8.refs_4_ = f32[2,216,864]{2,1,0:T(8,128)S(1)} custom-call(s32[1]{0:T(128)} %bitcast.refs_0_.share_ref, s32[1]{0:T(128)S(6)} %copy.18.refs_1_.transfer_ref, f32[24,128]{1,0:T(8,128)S(1)} %get-tuple-element.19.refs_2_.odd_freq_ref, bf16[4,136,128]{2,1,0:T(8,128)(2,1)S(1)} %collective-permute-done.4.refs_3_, ...), custom_call_target="tpu_custom_call", output_to_operand_aliasing={{}: (4, {})} | custom-call | flops 1800000000 | bytes 160000 | tf_op jit(solution)/shard_map/absorb/pallas_call | solution.py:226
  20.7 0.8 %collective-permute-done.3.refs_3_ = bf16[4,136,128]{2,1,0:T(8,128)(2,1)S(1)} collective-permute-done((bf16[4,136,128]{2,1,0:T(8,128)(2,1)S(1)}, bf16[4,136,128]{2,1,0:T(8,128)(2,1)S(1)}, u32[]{:S(2)}, u32[]{:S(2)}) %collective-permute-start.3) | collective-permute-done | bytes 139296 | tf_op jit(solution)/shard_map/ppermute | solution.py:251
  21.5 0.9 %collective-permute-start.5 = (bf16[4,136,128]{2,1,0:T(8,128)(2,1)S(1)}, bf16[4,136,128]{2,1,0:T(8,128)(2,1)S(1)}, u32[]{:S(2)}, u32[]{:S(2)}) collective-permute-start(bf16[4,136,128]{2,1,0:T(8,128)(2,1)S(1)} %collective-permute-done.3.refs_3_), channel_id=1, source_target_pairs={{1,0},{0,1},{3,2},{2,3},{5,4},{4,5},{7,6},{6,7},{9,8},{8,9},{11,10... | collective-permute-start | bytes 417800 | tf_op jit(solution)/shard_map/ppermute | solution.py:251
  22.3 2.9 %absorb.9.old_ref = f32[2,216,864]{2,1,0:T(8,128)S(1)} custom-call(s32[1]{0:T(128)} %bitcast.refs_0_.share_ref, s32[1]{0:T(128)S(6)} %copy.18.refs_1_.transfer_ref, f32[24,128]{1,0:T(8,128)S(1)} %get-tuple-element.19.refs_2_.odd_freq_ref, bf16[4,136,128]{2,1,0:T(8,128)(2,1)S(1)} %collective-permute-done.3.refs_3_, ...), custom_call_target="tpu_custom_call", output_to_operand_aliasing={{}: (4, {})} | custom-call | flops 1800000000 | bytes 160000 | tf_op jit(solution)/shard_map/absorb/pallas_call | solution.py:226
  25.2 0.0 collective-permute-done.5.walkers_ref
  25.3 3.7 %finish.1 = (f32[2,216,864]{2,1,0:T(8,128)S(1)}, f32[2,216,864]{2,1,0:T(8,128)}) custom-call(s32[1]{0:T(128)} %bitcast.refs_0_.share_ref, s32[1]{0:T(128)S(6)} %copy.18.refs_1_.transfer_ref, f32[24,128]{1,0:T(8,128)S(1)} %get-tuple-element.19.refs_2_.odd_freq_ref, ...), custom_call_target="tpu_custom_call", output_to_operand_aliasing={{0}: (4, {})} | custom-call | flops 1800000000 | bytes 160000 | tf_op jit(solution)/shard_map/finish/pallas_call | solution.py:226
  (4 shorter events, 0.0 us)
Async XLA Ops:
  0.9 7.5 %collective-permute-start.1 = (bf16[1,136,128]{2,1,0:T(8,128)(2,1)S(1)}, bf16[1,136,128]{2,1,0:T(8,128)(2,1)S(1)}, u32[]{:S(2)}, u32[]{:S(2)}) collective-permute-start(bf16[1,136,128]{2,1,0:T(8,128)(2,1)S(1)} %get-tuple-element.20.refs_3_), channel_id=1, source_target_pairs={{120,0},{121,1},{122,2},{123,3},{124,4},{125,5},{126,6},{127,7},{0... | collective-permute-start | bytes 104456 | tf_op jit(solution)/shard_map/ppermute | solution.py:251
  3.1 5.3 %collective-permute-start = (bf16[1,136,128]{2,1,0:T(8,128)(2,1)S(1)}, bf16[1,136,128]{2,1,0:T(8,128)(2,1)S(1)}, u32[]{:S(2)}, u32[]{:S(2)}) collective-permute-start(bf16[1,136,128]{2,1,0:T(8,128)(2,1)S(1)} %get-tuple-element.20.refs_3_), channel_id=1, source_target_pairs={{8,0},{9,1},{10,2},{11,3},{12,4},{13,5},{14,6},{15,7},{16,8},{17,9... | collective-permute-start | bytes 104456 | tf_op jit(solution)/shard_map/ppermute | solution.py:251
  8.4 5.5 %collective-permute-start.2 = (bf16[2,136,128]{2,1,0:T(8,128)(2,1)S(1)}, bf16[2,136,128]{2,1,0:T(8,128)(2,1)S(1)}, u32[]{:S(2)}, u32[]{:S(2)}) collective-permute-start(bf16[2,136,128]{2,1,0:T(8,128)(2,1)S(1)} %pad_maximum_fusion), channel_id=1, source_target_pairs={{6,0},{7,1},{4,2},{5,3},{2,4},{3,5},{0,6},{1,7},{14,8},{15,9},{12,... | collective-permute-start | bytes 208904 | tf_op jit(solution)/shard_map/ppermute | solution.py:251
  13.9 3.8 %collective-permute-start.4 = (bf16[4,136,128]{2,1,0:T(8,128)(2,1)S(1)}, bf16[4,136,128]{2,1,0:T(8,128)(2,1)S(1)}, u32[]{:S(2)}, u32[]{:S(2)}) collective-permute-start(bf16[4,136,128]{2,1,0:T(8,128)(2,1)S(1)} %constant_dynamic-update-slice_fusion), channel_id=1, source_target_pairs={{1,0},{0,1},{3,2},{2,3},{5,4},{4,5},{7,6},{6,7},{9,8},{8,9},{11,10... | collective-permute-start | bytes 417800 | tf_op jit(solution)/shard_map/ppermute | solution.py:251
  16.2 5.2 %collective-permute-start.3 = (bf16[4,136,128]{2,1,0:T(8,128)(2,1)S(1)}, bf16[4,136,128]{2,1,0:T(8,128)(2,1)S(1)}, u32[]{:S(2)}, u32[]{:S(2)}) collective-permute-start(bf16[4,136,128]{2,1,0:T(8,128)(2,1)S(1)} %constant_dynamic-update-slice_fusion), channel_id=1, source_target_pairs={{2,0},{3,1},{0,2},{1,3},{6,4},{7,5},{4,6},{5,7},{10,8},{11,9},{8,1... | collective-permute-start | bytes 417800 | tf_op jit(solution)/shard_map/ppermute | solution.py:251
  21.5 3.8 %collective-permute-start.5 = (bf16[4,136,128]{2,1,0:T(8,128)(2,1)S(1)}, bf16[4,136,128]{2,1,0:T(8,128)(2,1)S(1)}, u32[]{:S(2)}, u32[]{:S(2)}) collective-permute-start(bf16[4,136,128]{2,1,0:T(8,128)(2,1)S(1)} %collective-permute-done.3.refs_3_), channel_id=1, source_target_pairs={{1,0},{0,1},{3,2},{2,3},{5,4},{4,5},{7,6},{6,7},{9,8},{8,9},{11,10... | collective-permute-start | bytes 417800 | tf_op jit(solution)/shard_map/ppermute | solution.py:251

commit v4 on v3

--- a/solution.py
+++ b/solution.py
@@ -82,8 +82,13 @@
         st["flip_x"] = 1.0 - 2.0 * (site_x - 2.0 * jnp.floor(site_x * 0.5))
         st["flip_y"] = 1.0 - 2.0 * (site_y - 2.0 * jnp.floor(site_y * 0.5))
         matrix = walkers_ref[w, :V, :]
-        st["first"] = jnp.dot(stacked(*moved), matrix, preferred_element_type=jnp.float32)
-        st["second"] = lax.dot_general(stacked(*mine), matrix, (((1,), (1,)), ((), ())), preferred_element_type=jnp.float32)
+        zero = jnp.zeros_like(matrix)
+        weights = jnp.concatenate(
+            [jnp.concatenate([matrix, zero], axis=1), jnp.concatenate([zero, matrix.T], axis=1)], axis=0
+        )
+        both = jnp.concatenate([stacked(*moved), stacked(*mine)], axis=1)
+        both = jnp.dot(both, weights, preferred_element_type=jnp.float32)
+        st["first"], st["second"] = both[:, 0:V], both[:, V:]
 
     def p1():
         base_c, base_s = st["base"]
@@ -115,11 +120,18 @@
 
 def tile_main(t, table_ref, left_ref, acc_ref):
     start, size = COL_TILES[t]
-    product = lax.dot_general(left_ref[...], table_ref[pl.ds(start, size), :], (((1,), (1,)), ((), ())), preferred_element_type=jnp.float32)
-    product = product.reshape(27, 4, 8, size)
-    m_re, m_im, n_re, n_im = (product[:, i] for i in range(4))
-    acc_ref[0, :, pl.ds(start, size)] += (m_re * n_re - m_im * n_im).reshape(ROWS, size)
-    acc_ref[1, :, pl.ds(start, size)] += (m_re * n_im + m_im * n_re).reshape(ROWS, size)
+    cols = pl.ds(start, size)
+    for chunk in range(3):
+        product = lax.dot_general(
+            left_ref[pl.ds(288 * chunk, 288), :],
+            table_ref[cols, :],
+            (((1,), (1,)), ((), ())),
+            preferred_element_type=jnp.float32,
+        ).reshape(9, 4, 8, size)
+        m_re, m_im, n_re, n_im = (product[:, i] for i in range(4))
+        rows = pl.ds(72 * chunk, 72)
+        acc_ref[0, rows, cols] += (m_re * n_re - m_im * n_im).reshape(72, size)
+        acc_ref[1, rows, cols] += (m_re * n_im + m_im * n_re).reshape(72, size)
 
 
 def pack_kernel(freq_hbm, matrix_hbm, times_hbm, labels_hbm, packed_ref, odd_freq_ref, freq_ref, times_ref, labels_ref, sem):

time: 29.3 us -> 28.7 us (0.980)
  Pallas kernels: 13.7 us -> 12.8 us
  waiting for transfers between devices: 1.58 us -> 1.93 us
    pallas_call x6, Pallas kernels: 12.9 us -> 11.9 us  [absorb(): pl.pallas_call(finish_kernel if final else lambda *refs: absorb_kernel(ac...]
    ppermute x6, waiting for transfers between devices: 1.58 us -> 1.93 us  [permute(): return lax.ppermute(value, COORDS, pairs)]
  transfers between devices with their start and end apart: 6 -> 6, of which waited for: 2 -> 2; matrix products, arithmetic and copies ran while one was open for 0% -> 0% of each run, Pallas kernels for 31% -> 30%
where the time goes in v4:
time: 28.7 us; the launch traced here: 28.6 us
  starting transfers between devices  12.9 us (45%)
  Pallas kernels  12.8 us (45%)
  waiting for transfers between devices  1.93 us (7%)
  between operations  0.89 us (3%)
    ppermute x6, starting transfers between devices, permute(): return lax.ppermute(value, COORDS, pairs)  12.9 us
    pallas_call x6, Pallas kernels, absorb(): pl.pallas_call(finish_kernel if final else lambda *refs: absorb_kernel(ac...  11.9 us
    ppermute x6, waiting for transfers between devices, permute(): return lax.ppermute(value, COORDS, pairs)  1.93 us
    pallas_call x1, Pallas kernels, pack(): pl.pallas_call(pack_kernel, out_shape=(jax.ShapeDtypeStruct((1, PACK, V),...  0.86 us
  transfers between devices with their start and end apart: 6, of which 2 were waited for; matrix products, arithmetic and copies ran while one was open for 0% of the time, Pallas kernels for 30%

profile of v4, /device:TPU:1, one launch (start us, length us, event | category | flops | bytes accessed | tf_op | source)
XLA Modules:
  0.0 28.6 jit_solution(7873532732824607520)
XLA Ops:
  0.0 0.9 %pack.1 = (bf16[1,136,128]{2,1,0:T(8,128)(2,1)S(1)}, f32[24,128]{1,0:T(8,128)S(1)}) custom-call(s32[24]{0:T(128)} %freq_hbm.1, bf16[1,1,128,128]{3,2,1,0:T(8,128)(2,1)} %matrix_hbm.1, s32[1,1,128]{2,1,0:T(1,128)} %times_hbm.1, s32[1,1,128]{2,1,0:T(1,128)} %labels_hbm.1), custom_call_target="tpu_custom_call" | custom-call | tf_op jit(solution)/shard_map/pack/pallas_call | solution.py:163
  0.9 2.2 %collective-permute-start.1 = (bf16[1,136,128]{2,1,0:T(8,128)(2,1)S(1)}, bf16[1,136,128]{2,1,0:T(8,128)(2,1)S(1)}, u32[]{:S(2)}, u32[]{:S(2)}) collective-permute-start(bf16[1,136,128]{2,1,0:T(8,128)(2,1)S(1)} %get-tuple-element.20.refs_3_), channel_id=1, source_target_pairs={{120,0},{121,1},{122,2},{123,3},{124,4},{125,5},{126,6},{127,7},{0... | collective-permute-start | bytes 104456 | tf_op jit(solution)/shard_map/ppermute | solution.py:263
  3.1 3.7 %collective-permute-start = (bf16[1,136,128]{2,1,0:T(8,128)(2,1)S(1)}, bf16[1,136,128]{2,1,0:T(8,128)(2,1)S(1)}, u32[]{:S(2)}, u32[]{:S(2)}) collective-permute-start(bf16[1,136,128]{2,1,0:T(8,128)(2,1)S(1)} %get-tuple-element.20.refs_3_), channel_id=1, source_target_pairs={{8,0},{9,1},{10,2},{11,3},{12,4},{13,5},{14,6},{15,7},{16,8},{17,9... | collective-permute-start | bytes 104456 | tf_op jit(solution)/shard_map/ppermute | solution.py:263
  7.4 0.9 %absorb.5.refs_4_ = f32[2,216,864]{2,1,0:T(8,128)S(1)} custom-call(s32[1]{0:T(128)} %bitcast.refs_0_.share_ref, s32[1]{0:T(128)S(6)} %copy.18.refs_1_.transfer_ref, f32[24,128]{1,0:T(8,128)S(1)} %get-tuple-element.19.refs_2_.odd_freq_ref, bf16[1,136,128]{2,1,0:T(8,128)(2,1)S(1)} %get-tuple-element.20.refs_3_), custom_call_target="tpu_custom_call" | custom-call | flops 450000000 | bytes 40000 | tf_op jit(solution)/shard_map/absorb/pallas_call | solution.py:238
  8.3 0.0 collective-permute-done.1
  8.3 0.0 collective-permute-done.refs_3_
  8.4 3.8 %collective-permute-start.2 = (bf16[2,136,128]{2,1,0:T(8,128)(2,1)S(1)}, bf16[2,136,128]{2,1,0:T(8,128)(2,1)S(1)}, u32[]{:S(2)}, u32[]{:S(2)}) collective-permute-start(bf16[2,136,128]{2,1,0:T(8,128)(2,1)S(1)} %pad_maximum_fusion), channel_id=1, source_target_pairs={{6,0},{7,1},{4,2},{5,3},{2,4},{3,5},{0,6},{1,7},{14,8},{15,9},{12,... | collective-permute-start | bytes 208904 | tf_op jit(solution)/shard_map/ppermute | solution.py:263
  12.2 0.9 %absorb.6.refs_4_ = f32[2,216,864]{2,1,0:T(8,128)S(1)} custom-call(s32[1]{0:T(128)} %bitcast.refs_0_.share_ref, s32[1]{0:T(128)S(6)} %copy.18.refs_1_.transfer_ref, f32[24,128]{1,0:T(8,128)S(1)} %get-tuple-element.19.refs_2_.odd_freq_ref, bf16[1,136,128]{2,1,0:T(8,128)(2,1)S(1)} %collective-permute-done.refs_3_, ...), custom_call_target="tpu_custom_call", output_to_operand_aliasing={{}: (4, {})} | custom-call | flops 450000000 | bytes 40000 | tf_op jit(solution)/shard_map/absorb/pallas_call | solution.py:238
  13.1 0.8 %collective-permute-done.2.refs_3_ = bf16[2,136,128]{2,1,0:T(8,128)(2,1)S(1)} collective-permute-done((bf16[2,136,128]{2,1,0:T(8,128)(2,1)S(1)}, bf16[2,136,128]{2,1,0:T(8,128)(2,1)S(1)}, u32[]{:S(2)}, u32[]{:S(2)}) %collective-permute-start.2) | collective-permute-done | bytes 69664 | tf_op jit(solution)/shard_map/ppermute | solution.py:263
  14.0 2.3 %collective-permute-start.4 = (bf16[4,136,128]{2,1,0:T(8,128)(2,1)S(1)}, bf16[4,136,128]{2,1,0:T(8,128)(2,1)S(1)}, u32[]{:S(2)}, u32[]{:S(2)}) collective-permute-start(bf16[4,136,128]{2,1,0:T(8,128)(2,1)S(1)} %constant_dynamic-update-slice_fusion), channel_id=1, source_target_pairs={{1,0},{0,1},{3,2},{2,3},{5,4},{4,5},{7,6},{6,7},{9,8},{8,9},{11,10... | collective-permute-start | bytes 417800 | tf_op jit(solution)/shard_map/ppermute | solution.py:263
  16.2 0.0 collective-permute-start.3
  16.2 1.4 %absorb.7.refs_4_ = f32[2,216,864]{2,1,0:T(8,128)S(1)} custom-call(s32[1]{0:T(128)} %bitcast.refs_0_.share_ref, s32[1]{0:T(128)S(6)} %copy.18.refs_1_.transfer_ref, f32[24,128]{1,0:T(8,128)S(1)} %get-tuple-element.19.refs_2_.odd_freq_ref, bf16[2,136,128]{2,1,0:T(8,128)(2,1)S(1)} %collective-permute-done.2.refs_3_, ...), custom_call_target="tpu_custom_call", output_to_operand_aliasing={{}: (4, {})} | custom-call | flops 900000000 | bytes 80000 | tf_op jit(solution)/shard_map/absorb/pallas_call | solution.py:238
  17.7 0.0 collective-permute-done.4.refs_3_
  17.7 2.6 %absorb.8.refs_4_ = f32[2,216,864]{2,1,0:T(8,128)S(1)} custom-call(s32[1]{0:T(128)} %bitcast.refs_0_.share_ref, s32[1]{0:T(128)S(6)} %copy.18.refs_1_.transfer_ref, f32[24,128]{1,0:T(8,128)S(1)} %get-tuple-element.19.refs_2_.odd_freq_ref, bf16[4,136,128]{2,1,0:T(8,128)(2,1)S(1)} %collective-permute-done.4.refs_3_, ...), custom_call_target="tpu_custom_call", output_to_operand_aliasing={{}: (4, {})} | custom-call | flops 1800000000 | bytes 160000 | tf_op jit(solution)/shard_map/absorb/pallas_call | solution.py:238
  20.3 1.1 %collective-permute-done.3.refs_3_ = bf16[4,136,128]{2,1,0:T(8,128)(2,1)S(1)} collective-permute-done((bf16[4,136,128]{2,1,0:T(8,128)(2,1)S(1)}, bf16[4,136,128]{2,1,0:T(8,128)(2,1)S(1)}, u32[]{:S(2)}, u32[]{:S(2)}) %collective-permute-start.3) | collective-permute-done | bytes 139296 | tf_op jit(solution)/shard_map/ppermute | solution.py:263
  21.5 0.9 %collective-permute-start.5 = (bf16[4,136,128]{2,1,0:T(8,128)(2,1)S(1)}, bf16[4,136,128]{2,1,0:T(8,128)(2,1)S(1)}, u32[]{:S(2)}, u32[]{:S(2)}) collective-permute-start(bf16[4,136,128]{2,1,0:T(8,128)(2,1)S(1)} %collective-permute-done.3.refs_3_), channel_id=1, source_target_pairs={{1,0},{0,1},{3,2},{2,3},{5,4},{4,5},{7,6},{6,7},{9,8},{8,9},{11,10... | collective-permute-start | bytes 417800 | tf_op jit(solution)/shard_map/ppermute | solution.py:263
  22.3 2.6 %absorb.9.old_ref = f32[2,216,864]{2,1,0:T(8,128)S(1)} custom-call(s32[1]{0:T(128)} %bitcast.refs_0_.share_ref, s32[1]{0:T(128)S(6)} %copy.18.refs_1_.transfer_ref, f32[24,128]{1,0:T(8,128)S(1)} %get-tuple-element.19.refs_2_.odd_freq_ref, bf16[4,136,128]{2,1,0:T(8,128)(2,1)S(1)} %collective-permute-done.3.refs_3_, ...), custom_call_target="tpu_custom_call", output_to_operand_aliasing={{}: (4, {})} | custom-call | flops 1800000000 | bytes 160000 | tf_op jit(solution)/shard_map/absorb/pallas_call | solution.py:238
  25.0 0.0 collective-permute-done.5.walkers_ref
  25.0 3.4 %finish.1 = (f32[2,216,864]{2,1,0:T(8,128)S(1)}, f32[2,216,864]{2,1,0:T(8,128)}) custom-call(s32[1]{0:T(128)} %bitcast.refs_0_.share_ref, s32[1]{0:T(128)S(6)} %copy.18.refs_1_.transfer_ref, f32[24,128]{1,0:T(8,128)S(1)} %get-tuple-element.19.refs_2_.odd_freq_ref, ...), custom_call_target="tpu_custom_call", output_to_operand_aliasing={{0}: (4, {})} | custom-call | flops 1800000000 | bytes 160000 | tf_op jit(solution)/shard_map/finish/pallas_call | solution.py:238
  (4 shorter events, 0.0 us)
Async XLA Ops:
  0.9 7.5 %collective-permute-start.1 = (bf16[1,136,128]{2,1,0:T(8,128)(2,1)S(1)}, bf16[1,136,128]{2,1,0:T(8,128)(2,1)S(1)}, u32[]{:S(2)}, u32[]{:S(2)}) collective-permute-start(bf16[1,136,128]{2,1,0:T(8,128)(2,1)S(1)} %get-tuple-element.20.refs_3_), channel_id=1, source_target_pairs={{120,0},{121,1},{122,2},{123,3},{124,4},{125,5},{126,6},{127,7},{0... | collective-permute-start | bytes 104456 | tf_op jit(solution)/shard_map/ppermute | solution.py:263
  3.1 5.3 %collective-permute-start = (bf16[1,136,128]{2,1,0:T(8,128)(2,1)S(1)}, bf16[1,136,128]{2,1,0:T(8,128)(2,1)S(1)}, u32[]{:S(2)}, u32[]{:S(2)}) collective-permute-start(bf16[1,136,128]{2,1,0:T(8,128)(2,1)S(1)} %get-tuple-element.20.refs_3_), channel_id=1, source_target_pairs={{8,0},{9,1},{10,2},{11,3},{12,4},{13,5},{14,6},{15,7},{16,8},{17,9... | collective-permute-start | bytes 104456 | tf_op jit(solution)/shard_map/ppermute | solution.py:263
  8.4 5.5 %collective-permute-start.2 = (bf16[2,136,128]{2,1,0:T(8,128)(2,1)S(1)}, bf16[2,136,128]{2,1,0:T(8,128)(2,1)S(1)}, u32[]{:S(2)}, u32[]{:S(2)}) collective-permute-start(bf16[2,136,128]{2,1,0:T(8,128)(2,1)S(1)} %pad_maximum_fusion), channel_id=1, source_target_pairs={{6,0},{7,1},{4,2},{5,3},{2,4},{3,5},{0,6},{1,7},{14,8},{15,9},{12,... | collective-permute-start | bytes 208904 | tf_op jit(solution)/shard_map/ppermute | solution.py:263
  14.0 3.7 %collective-permute-start.4 = (bf16[4,136,128]{2,1,0:T(8,128)(2,1)S(1)}, bf16[4,136,128]{2,1,0:T(8,128)(2,1)S(1)}, u32[]{:S(2)}, u32[]{:S(2)}) collective-permute-start(bf16[4,136,128]{2,1,0:T(8,128)(2,1)S(1)} %constant_dynamic-update-slice_fusion), channel_id=1, source_target_pairs={{1,0},{0,1},{3,2},{2,3},{5,4},{4,5},{7,6},{6,7},{9,8},{8,9},{11,10... | collective-permute-start | bytes 417800 | tf_op jit(solution)/shard_map/ppermute | solution.py:263
  16.2 5.2 %collective-permute-start.3 = (bf16[4,136,128]{2,1,0:T(8,128)(2,1)S(1)}, bf16[4,136,128]{2,1,0:T(8,128)(2,1)S(1)}, u32[]{:S(2)}, u32[]{:S(2)}) collective-permute-start(bf16[4,136,128]{2,1,0:T(8,128)(2,1)S(1)} %constant_dynamic-update-slice_fusion), channel_id=1, source_target_pairs={{2,0},{3,1},{0,2},{1,3},{6,4},{7,5},{4,6},{5,7},{10,8},{11,9},{8,1... | collective-permute-start | bytes 417800 | tf_op jit(solution)/shard_map/ppermute | solution.py:263
  21.5 3.5 %collective-permute-start.5 = (bf16[4,136,128]{2,1,0:T(8,128)(2,1)S(1)}, bf16[4,136,128]{2,1,0:T(8,128)(2,1)S(1)}, u32[]{:S(2)}, u32[]{:S(2)}) collective-permute-start(bf16[4,136,128]{2,1,0:T(8,128)(2,1)S(1)} %collective-permute-done.3.refs_3_), channel_id=1, source_target_pairs={{1,0},{0,1},{3,2},{2,3},{5,4},{4,5},{7,6},{6,7},{9,8},{8,9},{11,10... | collective-permute-start | bytes 417800 | tf_op jit(solution)/shard_map/ppermute | solution.py:263

commit v5 on v4

--- a/solution.py
+++ b/solution.py
@@ -282,23 +282,33 @@
     def add(walkers, acc=None, final=False):
         return absorb(share, q_index, odd_freq, walkers, acc, final)
 
+    def flip_zl(x, y, zh, zl, core):
+        return x, y, zh, 1 - zl, core
+
+    def flip_core(x, y, zh, zl, core):
+        return x, y, zh, zl, 1 - core
+
+    def flip_z(x, y, zh, zl, core):
+        return x, y, 1 - zh, 1 - zl, core
+
     behind = permute(own, owner_at(-2))
     ahead = permute(own, owner_at(2))
+    early = permute(own, flip_zl)
     acc = add(own)
-    ahead, behind, acc = after(ahead, behind, acc)
+    ahead, behind, early, acc = after(ahead, behind, early, acc)
     odd_owner = lax.axis_index("zh") == 1
     send = jnp.concatenate([own, jnp.where(odd_owner, behind, ahead)], axis=0)
-    other = permute(send, lambda x, y, zh, zl, core: (x, y, 1 - zh, 1 - zl, core))
-    acc = add(ahead, acc)
+    other = permute(send, flip_z)
+    acc = add(jnp.concatenate([early, ahead], axis=0), acc)
     other, acc = after(other, acc)
-    group = jnp.concatenate([own, ahead, other], axis=0)
-    near = permute(group, lambda x, y, zh, zl, core: (x, y, zh, 1 - zl, core))
-    group_far = permute(group, lambda x, y, zh, zl, core: (x, y, zh, zl, 1 - core))
+    group = jnp.concatenate([own, ahead, other, early], axis=0)
+    near = permute(group[1:4], flip_zl)
+    group_far = permute(group, flip_core)
     acc = add(other, acc)
     group_far, acc = after(group_far, acc)
     acc = add(group_far, acc)
     near, acc = after(near, acc)
-    near_far = permute(near, lambda x, y, zh, zl, core: (x, y, zh, zl, 1 - core))
+    near_far = permute(near, flip_core)
     acc = add(near, acc)
     near_far, acc = after(near_far, acc)
     return add(near_far, acc, True)[None]

time: 28.7 us -> 28.5 us (level)
  waiting for transfers between devices: 1.93 us -> 0.56 us
  Pallas kernels: 12.8 us -> 13.4 us
  starting transfers between devices: 12.9 us -> 13.4 us
    ppermute x6 -> x7, waiting for transfers between devices: 1.93 us -> 0.56 us  [permute(): return lax.ppermute(value, COORDS, pairs)]
    pallas_call x6, Pallas kernels: 11.9 us -> 12.5 us  [absorb(): pl.pallas_call(finish_kernel if final else lambda *refs: absorb_kernel(ac...]
    ppermute x6 -> x7, starting transfers between devices: 12.9 us -> 13.4 us  [permute(): return lax.ppermute(value, COORDS, pairs)]
  transfers between devices with their start and end apart: 6 -> 7, of which waited for: 2 -> 1; matrix products, arithmetic and copies ran while one was open for 0% -> 0% of each run, Pallas kernels for 30% -> 34%
where the time goes in v5:
time: 28.5 us; the launch traced here: 28.4 us
  Pallas kernels  13.4 us (47%)
  starting transfers between devices  13.4 us (47%)
  between operations  0.92 us (3%)
  waiting for transfers between devices  0.56 us (2%)
    ppermute x7, starting transfers between devices, permute(): return lax.ppermute(value, COORDS, pairs)  13.4 us
    pallas_call x6, Pallas kernels, absorb(): pl.pallas_call(finish_kernel if final else lambda *refs: absorb_kernel(ac...  12.5 us
    pallas_call x1, Pallas kernels, pack(): pl.pallas_call(pack_kernel, out_shape=(jax.ShapeDtypeStruct((1, PACK, V),...  0.86 us
  transfers between devices with their start and end apart: 7, of which 1 were waited for; matrix products, arithmetic and copies ran while one was open for 0% of the time, Pallas kernels for 34%

profile of v5, /device:TPU:1, one launch (start us, length us, event | category | flops | bytes accessed | tf_op | source)
XLA Modules:
  0.0 28.4 jit_solution(9849424446868157796)
XLA Ops:
  0.0 0.9 %pack.1 = (bf16[1,136,128]{2,1,0:T(8,128)(2,1)S(1)}, f32[24,128]{1,0:T(8,128)S(1)}) custom-call(s32[24]{0:T(128)} %freq_hbm.1, bf16[1,1,128,128]{3,2,1,0:T(8,128)(2,1)} %matrix_hbm.1, s32[1,1,128]{2,1,0:T(1,128)} %times_hbm.1, s32[1,1,128]{2,1,0:T(1,128)} %labels_hbm.1), custom_call_target="tpu_custom_call" | custom-call | tf_op jit(solution)/shard_map/pack/pallas_call | solution.py:163
  0.9 2.5 %collective-permute-start.2 = (bf16[1,136,128]{2,1,0:T(8,128)(2,1)S(1)}, bf16[1,136,128]{2,1,0:T(8,128)(2,1)S(1)}, u32[]{:S(2)}, u32[]{:S(2)}) collective-permute-start(bf16[1,136,128]{2,1,0:T(8,128)(2,1)S(1)} %get-tuple-element.21.refs_3_), channel_id=1, source_target_pairs={{2,0},{3,1},{0,2},{1,3},{6,4},{7,5},{4,6},{5,7},{10,8},{11,9},{8,1... | collective-permute-start | bytes 104456 | tf_op jit(solution)/shard_map/ppermute | solution.py:263
  3.4 1.3 %collective-permute-start.1 = (bf16[1,136,128]{2,1,0:T(8,128)(2,1)S(1)}, bf16[1,136,128]{2,1,0:T(8,128)(2,1)S(1)}, u32[]{:S(2)}, u32[]{:S(2)}) collective-permute-start(bf16[1,136,128]{2,1,0:T(8,128)(2,1)S(1)} %get-tuple-element.21.refs_3_), channel_id=1, source_target_pairs={{120,0},{121,1},{122,2},{123,3},{124,4},{125,5},{126,6},{127,7},{0... | collective-permute-start | bytes 104456 | tf_op jit(solution)/shard_map/ppermute | solution.py:263
  4.7 3.6 %collective-permute-start = (bf16[1,136,128]{2,1,0:T(8,128)(2,1)S(1)}, bf16[1,136,128]{2,1,0:T(8,128)(2,1)S(1)}, u32[]{:S(2)}, u32[]{:S(2)}) collective-permute-start(bf16[1,136,128]{2,1,0:T(8,128)(2,1)S(1)} %get-tuple-element.21.refs_3_), channel_id=1, source_target_pairs={{8,0},{9,1},{10,2},{11,3},{12,4},{13,5},{14,6},{15,7},{16,8},{17,9... | collective-permute-start | bytes 104456 | tf_op jit(solution)/shard_map/ppermute | solution.py:263
  9.0 0.9 %absorb.5.refs_4_ = f32[2,216,864]{2,1,0:T(8,128)S(1)} custom-call(s32[1]{0:T(128)} %bitcast.refs_0_.share_ref, s32[1]{0:T(128)S(6)} %copy.16.refs_1_.transfer_ref, f32[24,128]{1,0:T(8,128)S(1)} %get-tuple-element.20.refs_2_.odd_freq_ref, bf16[1,136,128]{2,1,0:T(8,128)(2,1)S(1)} %get-tuple-element.21.refs_3_), custom_call_target="tpu_custom_call" | custom-call | flops 450000000 | bytes 40000 | tf_op jit(solution)/shard_map/absorb/pallas_call | solution.py:238
  9.9 0.0 collective-permute-done.2
  9.9 0.0 collective-permute-done.1
  9.9 0.0 collective-permute-done
  10.0 2.4 %collective-permute-start.3 = (bf16[2,136,128]{2,1,0:T(8,128)(2,1)S(1)}, bf16[2,136,128]{2,1,0:T(8,128)(2,1)S(1)}, u32[]{:S(2)}, u32[]{:S(2)}) collective-permute-start(bf16[2,136,128]{2,1,0:T(8,128)(2,1)S(1)} %pad_maximum_fusion.2), channel_id=1, source_target_pairs={{6,0},{7,1},{4,2},{5,3},{2,4},{3,5},{0,6},{1,7},{14,8},{15,9},{12,... | collective-permute-start | bytes 208904 | tf_op jit(solution)/shard_map/ppermute | solution.py:263
  12.4 1.5 %absorb.6.refs_4_ = f32[2,216,864]{2,1,0:T(8,128)S(1)} custom-call(s32[1]{0:T(128)} %bitcast.refs_0_.share_ref, s32[1]{0:T(128)S(6)} %copy.16.refs_1_.transfer_ref, f32[24,128]{1,0:T(8,128)S(1)} %get-tuple-element.20.refs_2_.odd_freq_ref, bf16[2,136,128]{2,1,0:T(8,128)(2,1)S(1)} %pad_maximum_fusion.3.refs_3_, ...), custom_call_target="tpu_custom_call", output_to_operand_aliasing={{}: (4, {})} | custom-call | flops 900000000 | bytes 80000 | tf_op jit(solution)/shard_map/absorb/pallas_call | solution.py:238
  13.9 0.5 %collective-permute-done.3.refs_3_ = bf16[2,136,128]{2,1,0:T(8,128)(2,1)S(1)} collective-permute-done((bf16[2,136,128]{2,1,0:T(8,128)(2,1)S(1)}, bf16[2,136,128]{2,1,0:T(8,128)(2,1)S(1)}, u32[]{:S(2)}, u32[]{:S(2)}) %collective-permute-start.3) | collective-permute-done | bytes 69664 | tf_op jit(solution)/shard_map/ppermute | solution.py:263
  14.5 2.9 %collective-permute-start.5 = (bf16[5,136,128]{2,1,0:T(8,128)(2,1)S(1)}, bf16[5,136,128]{2,1,0:T(8,128)(2,1)S(1)}, u32[]{:S(2)}, u32[]{:S(2)}) collective-permute-start(bf16[5,136,128]{2,1,0:T(8,128)(2,1)S(1)} %pad_maximum_fusion), channel_id=1, source_target_pairs={{1,0},{0,1},{3,2},{2,3},{5,4},{4,5},{7,6},{6,7},{9,8},{8,9},{11,10... | collective-permute-start | bytes 522248 | tf_op jit(solution)/shard_map/ppermute | solution.py:263
  17.4 0.1 collective-permute-start.4
  17.5 1.5 %absorb.7.refs_4_ = f32[2,216,864]{2,1,0:T(8,128)S(1)} custom-call(s32[1]{0:T(128)} %bitcast.refs_0_.share_ref, s32[1]{0:T(128)S(6)} %copy.16.refs_1_.transfer_ref, f32[24,128]{1,0:T(8,128)S(1)} %get-tuple-element.20.refs_2_.odd_freq_ref, bf16[2,136,128]{2,1,0:T(8,128)(2,1)S(1)} %collective-permute-done.3.refs_3_, ...), custom_call_target="tpu_custom_call", output_to_operand_aliasing={{}: (4, {})} | custom-call | flops 900000000 | bytes 80000 | tf_op jit(solution)/shard_map/absorb/pallas_call | solution.py:238
  19.0 0.0 collective-permute-done.5.refs_3_
  19.1 3.4 %absorb.8.refs_4_ = f32[2,216,864]{2,1,0:T(8,128)S(1)} custom-call(s32[1]{0:T(128)} %bitcast.refs_0_.share_ref, s32[1]{0:T(128)S(6)} %copy.16.refs_1_.transfer_ref, f32[24,128]{1,0:T(8,128)S(1)} %get-tuple-element.20.refs_2_.odd_freq_ref, bf16[5,136,128]{2,1,0:T(8,128)(2,1)S(1)} %collective-permute-done.5.refs_3_, ...), custom_call_target="tpu_custom_call", output_to_operand_aliasing={{}: (4, {})} | custom-call | flops 2249999872 | bytes 200000 | tf_op jit(solution)/shard_map/absorb/pallas_call | solution.py:238
  22.5 0.0 collective-permute-done.4.refs_3_
  22.5 0.6 %collective-permute-start.6 = (bf16[3,136,128]{2,1,0:T(8,128)(2,1)S(1)}, bf16[3,136,128]{2,1,0:T(8,128)(2,1)S(1)}, u32[]{:S(2)}, u32[]{:S(2)}) collective-permute-start(bf16[3,136,128]{2,1,0:T(8,128)(2,1)S(1)} %collective-permute-done.4.refs_3_), channel_id=1, source_target_pairs={{1,0},{0,1},{3,2},{2,3},{5,4},{4,5},{7,6},{6,7},{9,8},{8,9},{11,10... | collective-permute-start | bytes 313352 | tf_op jit(solution)/shard_map/ppermute | solution.py:263
  23.1 2.2 %absorb.9.old_ref = f32[2,216,864]{2,1,0:T(8,128)S(1)} custom-call(s32[1]{0:T(128)} %bitcast.refs_0_.share_ref, s32[1]{0:T(128)S(6)} %copy.16.refs_1_.transfer_ref, f32[24,128]{1,0:T(8,128)S(1)} %get-tuple-element.20.refs_2_.odd_freq_ref, bf16[3,136,128]{2,1,0:T(8,128)(2,1)S(1)} %collective-permute-done.4.refs_3_, ...), custom_call_target="tpu_custom_call", output_to_operand_aliasing={{}: (4, {})} | custom-call | flops 1350000000 | bytes 120000 | tf_op jit(solution)/shard_map/absorb/pallas_call | solution.py:238
  25.2 0.0 collective-permute-done.6.walkers_ref
  25.2 3.0 %finish.1 = (f32[2,216,864]{2,1,0:T(8,128)S(1)}, f32[2,216,864]{2,1,0:T(8,128)}) custom-call(s32[1]{0:T(128)} %bitcast.refs_0_.share_ref, s32[1]{0:T(128)S(6)} %copy.16.refs_1_.transfer_ref, f32[24,128]{1,0:T(8,128)S(1)} %get-tuple-element.20.refs_2_.odd_freq_ref, ...), custom_call_target="tpu_custom_call", output_to_operand_aliasing={{0}: (4, {})} | custom-call | flops 1350000000 | bytes 120000 | tf_op jit(solution)/shard_map/finish/pallas_call | solution.py:238
  (5 shorter events, 0.1 us)
Async XLA Ops:
  0.9 9.0 %collective-permute-start.2 = (bf16[1,136,128]{2,1,0:T(8,128)(2,1)S(1)}, bf16[1,136,128]{2,1,0:T(8,128)(2,1)S(1)}, u32[]{:S(2)}, u32[]{:S(2)}) collective-permute-start(bf16[1,136,128]{2,1,0:T(8,128)(2,1)S(1)} %get-tuple-element.21.refs_3_), channel_id=1, source_target_pairs={{2,0},{3,1},{0,2},{1,3},{6,4},{7,5},{4,6},{5,7},{10,8},{11,9},{8,1... | collective-permute-start | bytes 104456 | tf_op jit(solution)/shard_map/ppermute | solution.py:263
  3.4 6.5 %collective-permute-start.1 = (bf16[1,136,128]{2,1,0:T(8,128)(2,1)S(1)}, bf16[1,136,128]{2,1,0:T(8,128)(2,1)S(1)}, u32[]{:S(2)}, u32[]{:S(2)}) collective-permute-start(bf16[1,136,128]{2,1,0:T(8,128)(2,1)S(1)} %get-tuple-element.21.refs_3_), channel_id=1, source_target_pairs={{120,0},{121,1},{122,2},{123,3},{124,4},{125,5},{126,6},{127,7},{0... | collective-permute-start | bytes 104456 | tf_op jit(solution)/shard_map/ppermute | solution.py:263
  4.7 5.2 %collective-permute-start = (bf16[1,136,128]{2,1,0:T(8,128)(2,1)S(1)}, bf16[1,136,128]{2,1,0:T(8,128)(2,1)S(1)}, u32[]{:S(2)}, u32[]{:S(2)}) collective-permute-start(bf16[1,136,128]{2,1,0:T(8,128)(2,1)S(1)} %get-tuple-element.21.refs_3_), channel_id=1, source_target_pairs={{8,0},{9,1},{10,2},{11,3},{12,4},{13,5},{14,6},{15,7},{16,8},{17,9... | collective-permute-start | bytes 104456 | tf_op jit(solution)/shard_map/ppermute | solution.py:263
  10.0 4.5 %collective-permute-start.3 = (bf16[2,136,128]{2,1,0:T(8,128)(2,1)S(1)}, bf16[2,136,128]{2,1,0:T(8,128)(2,1)S(1)}, u32[]{:S(2)}, u32[]{:S(2)}) collective-permute-start(bf16[2,136,128]{2,1,0:T(8,128)(2,1)S(1)} %pad_maximum_fusion.2), channel_id=1, source_target_pairs={{6,0},{7,1},{4,2},{5,3},{2,4},{3,5},{0,6},{1,7},{14,8},{15,9},{12,... | collective-permute-start | bytes 208904 | tf_op jit(solution)/shard_map/ppermute | solution.py:263
  14.5 4.6 %collective-permute-start.5 = (bf16[5,136,128]{2,1,0:T(8,128)(2,1)S(1)}, bf16[5,136,128]{2,1,0:T(8,128)(2,1)S(1)}, u32[]{:S(2)}, u32[]{:S(2)}) collective-permute-start(bf16[5,136,128]{2,1,0:T(8,128)(2,1)S(1)} %pad_maximum_fusion), channel_id=1, source_target_pairs={{1,0},{0,1},{3,2},{2,3},{5,4},{4,5},{7,6},{6,7},{9,8},{8,9},{11,10... | collective-permute-start | bytes 522248 | tf_op jit(solution)/shard_map/ppermute | solution.py:263
  17.4 5.1 %collective-permute-start.4 = (bf16[3,136,128]{2,1,0:T(8,128)(2,1)S(1)}, bf16[3,136,128]{2,1,0:T(8,128)(2,1)S(1)}, u32[]{:S(2)}, u32[]{:S(2)}) collective-permute-start(bf16[3,136,128]{2,1,0:T(8,128)(2,1)S(1)} %pad_maximum_fusion.1), channel_id=1, source_target_pairs={{2,0},{3,1},{0,2},{1,3},{6,4},{7,5},{4,6},{5,7},{10,8},{11,9},{8,1... | collective-permute-start | bytes 313352 | tf_op jit(solution)/shard_map/ppermute | solution.py:263
  22.5 2.7 %collective-permute-start.6 = (bf16[3,136,128]{2,1,0:T(8,128)(2,1)S(1)}, bf16[3,136,128]{2,1,0:T(8,128)(2,1)S(1)}, u32[]{:S(2)}, u32[]{:S(2)}) collective-permute-start(bf16[3,136,128]{2,1,0:T(8,128)(2,1)S(1)} %collective-permute-done.4.refs_3_), channel_id=1, source_target_pairs={{1,0},{0,1},{3,2},{2,3},{5,4},{4,5},{7,6},{6,7},{9,8},{8,9},{11,10... | collective-permute-start | bytes 313352 | tf_op jit(solution)/shard_map/ppermute | solution.py:263

commit v6 on v5

--- a/solution.py
+++ b/solution.py
@@ -294,15 +294,16 @@
     behind = permute(own, owner_at(-2))
     ahead = permute(own, owner_at(2))
     early = permute(own, flip_zl)
+    own_far = permute(own, flip_core)
     acc = add(own)
-    ahead, behind, early, acc = after(ahead, behind, early, acc)
+    ahead, behind, early, own_far, acc = after(ahead, behind, early, own_far, acc)
     odd_owner = lax.axis_index("zh") == 1
     send = jnp.concatenate([own, jnp.where(odd_owner, behind, ahead)], axis=0)
     other = permute(send, flip_z)
-    acc = add(jnp.concatenate([early, ahead], axis=0), acc)
+    acc = add(jnp.concatenate([early, ahead, own_far], axis=0), acc)
     other, acc = after(other, acc)
-    group = jnp.concatenate([own, ahead, other, early], axis=0)
-    near = permute(group[1:4], flip_zl)
+    group = jnp.concatenate([ahead, other, early], axis=0)
+    near = permute(group[0:3], flip_zl)
     group_far = permute(group, flip_core)
     acc = add(other, acc)
     group_far, acc = after(group_far, acc)

time: 28.5 us -> 28.2 us (0.989)
  waiting for transfers between devices: 0.56 us -> 0.23 us
  Pallas kernels: 13.4 us -> 13.1 us
  starting transfers between devices: 13.4 us -> 13.7 us
    ppermute x7 -> x8, waiting for transfers between devices: 0.56 us -> 0.23 us  [permute(): return lax.ppermute(value, COORDS, pairs)]
    ppermute x7 -> x8, starting transfers between devices: 13.4 us -> 13.7 us  [permute(): return lax.ppermute(value, COORDS, pairs)]
  transfers between devices with their start and end apart: 7 -> 8, of which waited for: 1 -> 1; matrix products, arithmetic and copies ran while one was open for 0% -> 0% of each run, Pallas kernels for 34% -> 33%
where the time goes in v6:
time: 28.2 us; the launch traced here: 28.1 us
  starting transfers between devices  13.7 us (49%)
  Pallas kernels  13.1 us (46%)
  between operations  0.93 us (3%)
    ppermute x8, starting transfers between devices, permute(): return lax.ppermute(value, COORDS, pairs)  13.7 us
    pallas_call x6, Pallas kernels, absorb(): pl.pallas_call(finish_kernel if final else lambda *refs: absorb_kernel(ac...  12.3 us
    pallas_call x1, Pallas kernels, pack(): pl.pallas_call(pack_kernel, out_shape=(jax.ShapeDtypeStruct((1, PACK, V),...  0.86 us
  transfers between devices with their start and end apart: 8, of which 1 were waited for; matrix products, arithmetic and copies ran while one was open for 0% of the time, Pallas kernels for 33%

profile of v6, /device:TPU:1, one launch (start us, length us, event | category | flops | bytes accessed | tf_op | source)
XLA Modules:
  0.0 28.1 jit_solution(15643737887260759681)
XLA Ops:
  0.0 0.9 %pack.1 = (bf16[1,136,128]{2,1,0:T(8,128)(2,1)S(1)}, f32[24,128]{1,0:T(8,128)S(1)}) custom-call(s32[24]{0:T(128)} %freq_hbm.1, bf16[1,1,128,128]{3,2,1,0:T(8,128)(2,1)} %matrix_hbm.1, s32[1,1,128]{2,1,0:T(1,128)} %times_hbm.1, s32[1,1,128]{2,1,0:T(1,128)} %labels_hbm.1), custom_call_target="tpu_custom_call" | custom-call | tf_op jit(solution)/shard_map/pack/pallas_call | solution.py:163
  0.9 1.5 %collective-permute-start.3 = (bf16[1,136,128]{2,1,0:T(8,128)(2,1)S(1)}, bf16[1,136,128]{2,1,0:T(8,128)(2,1)S(1)}, u32[]{:S(2)}, u32[]{:S(2)}) collective-permute-start(bf16[1,136,128]{2,1,0:T(8,128)(2,1)S(1)} %get-tuple-element.22.refs_3_), channel_id=1, source_target_pairs={{1,0},{0,1},{3,2},{2,3},{5,4},{4,5},{7,6},{6,7},{9,8},{8,9},{11,10... | collective-permute-start | bytes 104456 | tf_op jit(solution)/shard_map/ppermute | solution.py:263
  2.4 1.7 %collective-permute-start.2 = (bf16[1,136,128]{2,1,0:T(8,128)(2,1)S(1)}, bf16[1,136,128]{2,1,0:T(8,128)(2,1)S(1)}, u32[]{:S(2)}, u32[]{:S(2)}) collective-permute-start(bf16[1,136,128]{2,1,0:T(8,128)(2,1)S(1)} %get-tuple-element.22.refs_3_), channel_id=1, source_target_pairs={{2,0},{3,1},{0,2},{1,3},{6,4},{7,5},{4,6},{5,7},{10,8},{11,9},{8,1... | collective-permute-start | bytes 104456 | tf_op jit(solution)/shard_map/ppermute | solution.py:263
  4.1 1.3 %collective-permute-start.1 = (bf16[1,136,128]{2,1,0:T(8,128)(2,1)S(1)}, bf16[1,136,128]{2,1,0:T(8,128)(2,1)S(1)}, u32[]{:S(2)}, u32[]{:S(2)}) collective-permute-start(bf16[1,136,128]{2,1,0:T(8,128)(2,1)S(1)} %get-tuple-element.22.refs_3_), channel_id=1, source_target_pairs={{120,0},{121,1},{122,2},{123,3},{124,4},{125,5},{126,6},{127,7},{0... | collective-permute-start | bytes 104456 | tf_op jit(solution)/shard_map/ppermute | solution.py:263
  5.4 3.6 %collective-permute-start = (bf16[1,136,128]{2,1,0:T(8,128)(2,1)S(1)}, bf16[1,136,128]{2,1,0:T(8,128)(2,1)S(1)}, u32[]{:S(2)}, u32[]{:S(2)}) collective-permute-start(bf16[1,136,128]{2,1,0:T(8,128)(2,1)S(1)} %get-tuple-element.22.refs_3_), channel_id=1, source_target_pairs={{8,0},{9,1},{10,2},{11,3},{12,4},{13,5},{14,6},{15,7},{16,8},{17,9... | collective-permute-start | bytes 104456 | tf_op jit(solution)/shard_map/ppermute | solution.py:263
  9.7 0.9 %absorb.5.refs_4_ = f32[2,216,864]{2,1,0:T(8,128)S(1)} custom-call(s32[1]{0:T(128)} %bitcast.refs_0_.share_ref, s32[1]{0:T(128)S(6)} %copy.16.refs_1_.transfer_ref, f32[24,128]{1,0:T(8,128)S(1)} %get-tuple-element.21.refs_2_.odd_freq_ref, bf16[1,136,128]{2,1,0:T(8,128)(2,1)S(1)} %get-tuple-element.22.refs_3_), custom_call_target="tpu_custom_call" | custom-call | flops 450000000 | bytes 40000 | tf_op jit(solution)/shard_map/absorb/pallas_call | solution.py:238
  10.6 0.0 collective-permute-done.3
  10.6 0.0 collective-permute-done.2
  10.6 0.0 collective-permute-done.1
  10.6 0.0 collective-permute-done
  10.7 2.3 %collective-permute-start.4 = (bf16[2,136,128]{2,1,0:T(8,128)(2,1)S(1)}, bf16[2,136,128]{2,1,0:T(8,128)(2,1)S(1)}, u32[]{:S(2)}, u32[]{:S(2)}) collective-permute-start(bf16[2,136,128]{2,1,0:T(8,128)(2,1)S(1)} %pad_maximum_fusion.3), channel_id=1, source_target_pairs={{6,0},{7,1},{4,2},{5,3},{2,4},{3,5},{0,6},{1,7},{14,8},{15,9},{12,... | collective-permute-start | bytes 208904 | tf_op jit(solution)/shard_map/ppermute | solution.py:263
  13.0 2.1 %absorb.6.refs_4_ = f32[2,216,864]{2,1,0:T(8,128)S(1)} custom-call(s32[1]{0:T(128)} %bitcast.refs_0_.share_ref, s32[1]{0:T(128)S(6)} %copy.16.refs_1_.transfer_ref, f32[24,128]{1,0:T(8,128)S(1)} %get-tuple-element.21.refs_2_.odd_freq_ref, bf16[3,136,128]{2,1,0:T(8,128)(2,1)S(1)} %pad_maximum_fusion.1.refs_3_, ...), custom_call_target="tpu_custom_call", output_to_operand_aliasing={{}: (4, {})} | custom-call | flops 1350000000 | bytes 120000 | tf_op jit(solution)/shard_map/absorb/pallas_call | solution.py:238
  15.1 0.0 collective-permute-done.4.refs_3_
  15.2 2.3 %collective-permute-start.6 = (bf16[4,136,128]{2,1,0:T(8,128)(2,1)S(1)}, bf16[4,136,128]{2,1,0:T(8,128)(2,1)S(1)}, u32[]{:S(2)}, u32[]{:S(2)}) collective-permute-start(bf16[4,136,128]{2,1,0:T(8,128)(2,1)S(1)} %pad_maximum_fusion), channel_id=1, source_target_pairs={{1,0},{0,1},{3,2},{2,3},{5,4},{4,5},{7,6},{6,7},{9,8},{8,9},{11,10... | collective-permute-start | bytes 417800 | tf_op jit(solution)/shard_map/ppermute | solution.py:263
  17.5 0.1 collective-permute-start.5
  17.6 1.5 %absorb.7.refs_4_ = f32[2,216,864]{2,1,0:T(8,128)S(1)} custom-call(s32[1]{0:T(128)} %bitcast.refs_0_.share_ref, s32[1]{0:T(128)S(6)} %copy.16.refs_1_.transfer_ref, f32[24,128]{1,0:T(8,128)S(1)} %get-tuple-element.21.refs_2_.odd_freq_ref, bf16[2,136,128]{2,1,0:T(8,128)(2,1)S(1)} %collective-permute-done.4.refs_3_, ...), custom_call_target="tpu_custom_call", output_to_operand_aliasing={{}: (4, {})} | custom-call | flops 900000000 | bytes 80000 | tf_op jit(solution)/shard_map/absorb/pallas_call | solution.py:238
  19.1 0.0 collective-permute-done.6.refs_3_
  19.1 2.8 %absorb.8.refs_4_ = f32[2,216,864]{2,1,0:T(8,128)S(1)} custom-call(s32[1]{0:T(128)} %bitcast.refs_0_.share_ref, s32[1]{0:T(128)S(6)} %copy.16.refs_1_.transfer_ref, f32[24,128]{1,0:T(8,128)S(1)} %get-tuple-element.21.refs_2_.odd_freq_ref, bf16[4,136,128]{2,1,0:T(8,128)(2,1)S(1)} %collective-permute-done.6.refs_3_, ...), custom_call_target="tpu_custom_call", output_to_operand_aliasing={{}: (4, {})} | custom-call | flops 1800000000 | bytes 160000 | tf_op jit(solution)/shard_map/absorb/pallas_call | solution.py:238
  21.9 0.2 collective-permute-done.5.refs_3_
  22.1 0.8 %collective-permute-start.7 = (bf16[3,136,128]{2,1,0:T(8,128)(2,1)S(1)}, bf16[3,136,128]{2,1,0:T(8,128)(2,1)S(1)}, u32[]{:S(2)}, u32[]{:S(2)}) collective-permute-start(bf16[3,136,128]{2,1,0:T(8,128)(2,1)S(1)} %collective-permute-done.5.refs_3_), channel_id=1, source_target_pairs={{1,0},{0,1},{3,2},{2,3},{5,4},{4,5},{7,6},{6,7},{9,8},{8,9},{11,10... | collective-permute-start | bytes 313352 | tf_op jit(solution)/shard_map/ppermute | solution.py:263
  22.9 2.1 %absorb.9.old_ref = f32[2,216,864]{2,1,0:T(8,128)S(1)} custom-call(s32[1]{0:T(128)} %bitcast.refs_0_.share_ref, s32[1]{0:T(128)S(6)} %copy.16.refs_1_.transfer_ref, f32[24,128]{1,0:T(8,128)S(1)} %get-tuple-element.21.refs_2_.odd_freq_ref, bf16[3,136,128]{2,1,0:T(8,128)(2,1)S(1)} %collective-permute-done.5.refs_3_, ...), custom_call_target="tpu_custom_call", output_to_operand_aliasing={{}: (4, {})} | custom-call | flops 1350000000 | bytes 120000 | tf_op jit(solution)/shard_map/absorb/pallas_call | solution.py:238
  25.0 0.0 collective-permute-done.7.walkers_ref
  25.0 2.9 %finish.1 = (f32[2,216,864]{2,1,0:T(8,128)S(1)}, f32[2,216,864]{2,1,0:T(8,128)}) custom-call(s32[1]{0:T(128)} %bitcast.refs_0_.share_ref, s32[1]{0:T(128)S(6)} %copy.16.refs_1_.transfer_ref, f32[24,128]{1,0:T(8,128)S(1)} %get-tuple-element.21.refs_2_.odd_freq_ref, ...), custom_call_target="tpu_custom_call", output_to_operand_aliasing={{0}: (4, {})} | custom-call | flops 1350000000 | bytes 120000 | tf_op jit(solution)/shard_map/finish/pallas_call | solution.py:238
  (5 shorter events, 0.1 us)
Async XLA Ops:
  0.9 9.7 %collective-permute-start.3 = (bf16[1,136,128]{2,1,0:T(8,128)(2,1)S(1)}, bf16[1,136,128]{2,1,0:T(8,128)(2,1)S(1)}, u32[]{:S(2)}, u32[]{:S(2)}) collective-permute-start(bf16[1,136,128]{2,1,0:T(8,128)(2,1)S(1)} %get-tuple-element.22.refs_3_), channel_id=1, source_target_pairs={{1,0},{0,1},{3,2},{2,3},{5,4},{4,5},{7,6},{6,7},{9,8},{8,9},{11,10... | collective-permute-start | bytes 104456 | tf_op jit(solution)/shard_map/ppermute | solution.py:263
  2.4 8.2 %collective-permute-start.2 = (bf16[1,136,128]{2,1,0:T(8,128)(2,1)S(1)}, bf16[1,136,128]{2,1,0:T(8,128)(2,1)S(1)}, u32[]{:S(2)}, u32[]{:S(2)}) collective-permute-start(bf16[1,136,128]{2,1,0:T(8,128)(2,1)S(1)} %get-tuple-element.22.refs_3_), channel_id=1, source_target_pairs={{2,0},{3,1},{0,2},{1,3},{6,4},{7,5},{4,6},{5,7},{10,8},{11,9},{8,1... | collective-permute-start | bytes 104456 | tf_op jit(solution)/shard_map/ppermute | solution.py:263
  4.1 6.5 %collective-permute-start.1 = (bf16[1,136,128]{2,1,0:T(8,128)(2,1)S(1)}, bf16[1,136,128]{2,1,0:T(8,128)(2,1)S(1)}, u32[]{:S(2)}, u32[]{:S(2)}) collective-permute-start(bf16[1,136,128]{2,1,0:T(8,128)(2,1)S(1)} %get-tuple-element.22.refs_3_), channel_id=1, source_target_pairs={{120,0},{121,1},{122,2},{123,3},{124,4},{125,5},{126,6},{127,7},{0... | collective-permute-start | bytes 104456 | tf_op jit(solution)/shard_map/ppermute | solution.py:263
  5.4 5.2 %collective-permute-start = (bf16[1,136,128]{2,1,0:T(8,128)(2,1)S(1)}, bf16[1,136,128]{2,1,0:T(8,128)(2,1)S(1)}, u32[]{:S(2)}, u32[]{:S(2)}) collective-permute-start(bf16[1,136,128]{2,1,0:T(8,128)(2,1)S(1)} %get-tuple-element.22.refs_3_), channel_id=1, source_target_pairs={{8,0},{9,1},{10,2},{11,3},{12,4},{13,5},{14,6},{15,7},{16,8},{17,9... | collective-permute-start | bytes 104456 | tf_op jit(solution)/shard_map/ppermute | solution.py:263
  10.7 4.5 %collective-permute-start.4 = (bf16[2,136,128]{2,1,0:T(8,128)(2,1)S(1)}, bf16[2,136,128]{2,1,0:T(8,128)(2,1)S(1)}, u32[]{:S(2)}, u32[]{:S(2)}) collective-permute-start(bf16[2,136,128]{2,1,0:T(8,128)(2,1)S(1)} %pad_maximum_fusion.3), channel_id=1, source_target_pairs={{6,0},{7,1},{4,2},{5,3},{2,4},{3,5},{0,6},{1,7},{14,8},{15,9},{12,... | collective-permute-start | bytes 208904 | tf_op jit(solution)/shard_map/ppermute | solution.py:263
  15.2 3.9 %collective-permute-start.6 = (bf16[4,136,128]{2,1,0:T(8,128)(2,1)S(1)}, bf16[4,136,128]{2,1,0:T(8,128)(2,1)S(1)}, u32[]{:S(2)}, u32[]{:S(2)}) collective-permute-start(bf16[4,136,128]{2,1,0:T(8,128)(2,1)S(1)} %pad_maximum_fusion), channel_id=1, source_target_pairs={{1,0},{0,1},{3,2},{2,3},{5,4},{4,5},{7,6},{6,7},{9,8},{8,9},{11,10... | collective-permute-start | bytes 417800 | tf_op jit(solution)/shard_map/ppermute | solution.py:263
  17.5 4.6 %collective-permute-start.5 = (bf16[3,136,128]{2,1,0:T(8,128)(2,1)S(1)}, bf16[3,136,128]{2,1,0:T(8,128)(2,1)S(1)}, u32[]{:S(2)}, u32[]{:S(2)}) collective-permute-start(bf16[3,136,128]{2,1,0:T(8,128)(2,1)S(1)} %pad_maximum_fusion.2), channel_id=1, source_target_pairs={{2,0},{3,1},{0,2},{1,3},{6,4},{7,5},{4,6},{5,7},{10,8},{11,9},{8,1... | collective-permute-start | bytes 313352 | tf_op jit(solution)/shard_map/ppermute | solution.py:263
  22.1 2.9 %collective-permute-start.7 = (bf16[3,136,128]{2,1,0:T(8,128)(2,1)S(1)}, bf16[3,136,128]{2,1,0:T(8,128)(2,1)S(1)}, u32[]{:S(2)}, u32[]{:S(2)}) collective-permute-start(bf16[3,136,128]{2,1,0:T(8,128)(2,1)S(1)} %collective-permute-done.5.refs_3_), channel_id=1, source_target_pairs={{1,0},{0,1},{3,2},{2,3},{5,4},{4,5},{7,6},{6,7},{9,8},{8,9},{11,10... | collective-permute-start | bytes 313352 | tf_op jit(solution)/shard_map/ppermute | solution.py:263
